TPU v7x, 512 devices: a whole 4x8x8 slice. The times are simulated.
512 devices in a mesh: subtree: 32 (over x, y), front: 16 (over z, core).
Axes of the slice: x: 4, y: 8, z: 8, core: 2. Of those that a mesh axis runs over, the one named last changes fastest.
Arguments:
- modes_root: bfloat16 [1, 64, 12288], P(None, None, 'subtree'), may hold values from -6 to 6
- modes_mid: bfloat16 [2, 64, 8192], P(None, None, 'subtree'), may hold values from -6 to 6
- modes_low: bfloat16 [4, 64, 8192], P(None, None, 'subtree'), may hold values from -6 to 6
- factor_root: bfloat16 [1, 12288, 12288], P(None, 'front', 'subtree')
- factor_mid: bfloat16 [2, 8192, 8192], P(None, 'front', 'subtree')
- factor_low: bfloat16 [4, 8192, 8192], P(None, 'front', 'subtree')
- update_mid: bfloat16 [2, 4096, 8192], P(None, 'subtree', 'front'), may hold values from -0.0625 to 0.0625
- update_low: bfloat16 [4, 4096, 8192], P(None, 'subtree', 'front'), may hold values from -0.0625 to 0.0625
- map_mid: int32 [2, 32], P(None, 'subtree'), may hold values from 0 to 467, as said below
- map_low: int32 [4, 32], P(None, 'subtree'), may hold values from 0 to 471, as said below
- mass_vals: bfloat16 [480, 16, 128, 128], P('subtree', 'front'), may hold values from -0.125 to 0.125
- mass_cols: int32 [480, 16], P('subtree', 'front'), may hold values from 0 to 479, as said below
Outputs:
- solved_root: float32 [1, 64, 12288], P(None, None, 'subtree')
- solved_mid: float32 [2, 64, 8192], P(None, None, 'subtree')
- solved_low: float32 [4, 64, 8192], P(None, None, 'subtree')
- gram_stiff: float32 [64, 64], replicated
- gram_mass: float32 [64, 64], replicated
Inputs may be any that keep to these rules, and one draw needn't show every extreme that they name: Rows of map_mid: each node has exactly one update block per owner: entry c of node n names a block (owner-major numbering) of the root separator's slice of owner c. Rows of map_low: each node has exactly one update block per owner: entry c of node n names a block of owner c in that owner's slice of the root separator or of middle node n // 2. `mass_cols`: entry 0 of block row r is r itself; every entry names a block of the same owner as r or of the owner just before or after it.
All inputs are finite; a program needn't handle non-finite values.
Results may differ from a plain program's by a relative error of at most 0.035.
Values may be sent and summed in bfloat16 or wider, within the bound.
No kernel may reach another device: no remote copies, remote signals or barrier semaphores. Data moves between devices by JAX's collectives and lax.ppermute only.
A program may use at most 64 MiB of HBM per device.

v0:
```python
import functools

import jax
import jax.numpy as jnp
from jax import lax
from jax.experimental import pallas as pl
from jax.experimental.pallas import tpu as pltpu
from jax.sharding import Mesh, PartitionSpec as P


BLOCK = 128
F32 = jnp.float32
BF16 = jnp.bfloat16
FRONT = ("z", "core")


def total(parts):
    return jnp.sum(parts.astype(F32), axis=0)


def exchange(pieces, axis, held):
    return lax.optimization_barrier((lax.all_to_all(pieces, axis, 0, 0), *held))


def gather(piece, axis, *held):
    copies = jnp.broadcast_to(piece[None], (lax.axis_size(axis), *piece.shape))
    return exchange(copies, axis, held)


def scatter_sum(pieces, axis, *held):
    got, *held = exchange(pieces.astype(BF16), axis, held)
    return total(got), *held


def full_sum(part, axis, *held):
    got, *held = gather(part.astype(BF16), axis, *held)
    return total(got), *held


def swap(value):
    return lax.ppermute(value, "core", [(0, 1), (1, 0)])


def neighbours(flat):
    count = lax.axis_size("subtree")
    before = lax.ppermute(flat, "subtree", [(i, i + 1) for i in range(count - 1)])
    after = lax.ppermute(flat, "subtree", [(i + 1, i) for i in range(count - 1)])
    return before, after


def _lanes(width):
    return [slice(at, at + 256) for at in range(0, width, 256)]


def _run(moves, sems):
    copies = [pltpu.make_async_copy(*move, sems.at[i]) for i, move in enumerate(moves)]
    for copy in copies:
        copy.start()
    for copy in copies:
        copy.wait()


def _pack_kernel(core_ref, *refs, count):
    weights, sent, stacks = refs[:count], refs[count], refs[count + 1 : 2 * count + 1]
    staged, halves, sems = refs[2 * count + 1], refs[2 * count + 2 : -1], refs[-1]
    core = core_ref[0]
    moves = []
    row = 0
    for weight, half in zip(weights, halves):
        nodes, rows, width = half.shape
        moves.append((weight.at[pl.ds(core * nodes, nodes)], half))
        for node in range(nodes):
            for lanes in _lanes(width):
                source = weight.at[(1 - core) * nodes + node, :, lanes]
                moves.append((source, staged.at[row : row + rows]))
                row += rows
    _run(moves, sems)
    out = [(half, stack.at[0]) for half, stack in zip(halves, stacks)]
    _run([(staged, sent), *out], sems)


def _unpack_kernel(received, *refs, count):
    stacks, sems = refs[count : 2 * count], refs[-1]
    moves = []
    row = 0
    for stack in stacks:
        nodes, rows, width = stack.shape[1:]
        for node in range(nodes):
            for lanes in _lanes(width):
                moves.append((received.at[row : row + rows], stack.at[1, node, :, lanes]))
                row += rows
    _run(moves, sems)


def _side_by_side_kernel(*refs):
    levels, flat, sems = refs[:-2], refs[-2], refs[-1]
    moves = []
    at = 0
    for level in levels:
        nodes, _, width = level.shape
        for node in range(nodes):
            moves.append((level.at[node], flat.at[:, at : at + width]))
            at += width
    _run(moves, sems)


def side_by_side(*levels):
    width = sum(level.shape[0] * level.shape[2] for level in levels)
    return pl.pallas_call(
        _side_by_side_kernel,
        out_shape=jax.ShapeDtypeStruct((levels[0].shape[1], width), BF16),
        in_specs=[pl.BlockSpec(memory_space=pl.ANY)] * len(levels),
        out_specs=pl.BlockSpec(memory_space=pltpu.VMEM),
        scratch_shapes=[pltpu.SemaphoreType.DMA((sum(level.shape[0] for level in levels),))],
        name="side_by_side",
    )(*levels)


def split_nodes(core, *weights):
    count = len(weights)
    shapes = [(2, w.shape[0] // 2, *w.shape[1:]) for w in weights]
    crossing = sum(n * (width // 256) for _, n, _, width in shapes)
    rows = sum(n * r * (width // 256) for _, n, r, width in shapes)
    anywhere = pl.BlockSpec(memory_space=pl.ANY)
    sent, *stacks = pl.pallas_call(
        functools.partial(_pack_kernel, count=count),
        out_shape=[jax.ShapeDtypeStruct(shape, BF16) for shape in ((rows, 256), *shapes)],
        in_specs=[pl.BlockSpec(memory_space=pltpu.SMEM)] + [anywhere] * count,
        out_specs=[anywhere] * (count + 1),
        scratch_shapes=[
            pltpu.VMEM((rows, 256), BF16),
            *(pltpu.VMEM(shape[1:], BF16) for shape in shapes),
            pltpu.SemaphoreType.DMA((crossing + count,)),
        ],
        name="pack",
    )(core.reshape(1), *weights)
    return stacks, swap(sent)


def unpacked(stacks, received):
    count = len(stacks)
    crossing = sum(s.shape[1] * (s.shape[3] // 256) for s in stacks)
    anywhere = pl.BlockSpec(memory_space=pl.ANY)
    return pl.pallas_call(
        functools.partial(_unpack_kernel, count=count),
        out_shape=[jax.ShapeDtypeStruct(s.shape, BF16) for s in stacks],
        in_specs=[pl.BlockSpec(memory_space=pltpu.VMEM)] + [anywhere] * count,
        out_specs=[anywhere] * count,
        input_output_aliases={i + 1: i for i in range(count)},
        scratch_shapes=[pltpu.SemaphoreType.DMA((crossing,))],
        name="unpack",
    )(pltpu.with_memory_space_constraint(received, pltpu.VMEM), *stacks)


def to_pieces(value, count, width):
    lead = value.size // value.shape[-1] // 8
    blocks = value.reshape(lead, 8, -1, width).transpose(0, 2, 1, 3).reshape(-1, 8, width)
    spare = count - blocks.shape[0]
    if spare:
        blocks = jnp.concatenate([blocks, jnp.zeros((spare, 8, width), blocks.dtype)], axis=0)
    return blocks


def from_pieces(blocks, shape):
    width = blocks.shape[-1]
    across = shape[-1] // width
    lead = 1
    for size in shape[:-1]:
        lead *= size
    used = blocks[: lead // 8 * across]
    return used.reshape(lead // 8, across, 8, width).transpose(0, 2, 1, 3).reshape(shape)


def mass_partial(window, column, mass_vals):
    modes = window.shape[0]
    picked = window.reshape(modes, -1, BLOCK)[:, column, :]
    product = jnp.einsum("mrei,reoi->mro", picked, mass_vals, preferred_element_type=F32)
    return product.reshape(modes, -1)


def _unpaired_kernel(grams, stiff, mass, *, n_mass, n_stiff):
    modes = mass.shape[1]
    every = jnp.sum(grams[:, :n_mass, :].astype(F32), axis=0)
    mass[:n_mass] = every[:, :modes]
    mass[n_mass:] = every[:, modes:]
    for layer in range(grams.shape[0] // 2):
        rows = slice(n_mass, n_mass + 8)
        pair = grams[2 * layer, rows, :].astype(F32) + grams[2 * layer + 1, rows, :].astype(F32)
        at = 2 * n_stiff * layer
        stiff[at : at + n_stiff] = pair[:n_stiff, :modes]
        stiff[at + n_stiff : at + 2 * n_stiff] = pair[:n_stiff, modes:]


def unpaired(grams, n_mass, n_stiff):
    modes = grams.shape[2] // 2
    return pl.pallas_call(
        functools.partial(_unpaired_kernel, n_mass=n_mass, n_stiff=n_stiff),
        out_shape=[jax.ShapeDtypeStruct((modes, modes), F32)] * 2,
        in_specs=[pl.BlockSpec(memory_space=pltpu.VMEM)],
        name="unpaired",
    )(pltpu.with_memory_space_constraint(grams, pltpu.VMEM))


def per_device(
    modes_root,
    modes_mid,
    modes_low,
    factor_root,
    factor_mid,
    factor_low,
    update_mid,
    update_low,
    map_mid,
    map_low,
    mass_vals,
    mass_cols,
):
    owner = lax.axis_index("subtree")
    core = lax.axis_index("core")
    owners = lax.axis_size("subtree")
    layers = lax.axis_size("z")
    modes = modes_root.shape[1]
    w_root, w_mid, w_low = modes_root.shape[2], modes_mid.shape[2], modes_low.shape[2]
    b_root, b_mid, b_low = w_root // BLOCK, w_mid // BLOCK, w_low // BLOCK
    local_blocks = b_root + 2 * b_mid + 4 * b_low
    b_own = b_mid + 2 * b_low
    w_own = b_own * BLOCK
    mid_at, low_at = w_root, w_root + w_mid

    def half(value, which, axis=0):
        size = value.shape[axis] // 2
        return lax.dynamic_slice_in_dim(value, which * size, size, axis)

    column = mass_cols - (owner - 1) * local_blocks
    place = column // local_blocks
    block = column % local_blocks
    is_low = block >= b_root + 2 * b_mid
    after_root = block - b_root
    low_block = after_root - 2 * b_mid
    of = jnp.where(is_low, low_block // (2 * b_low), after_root // b_mid)
    within = jnp.where(is_low, b_mid + low_block % (2 * b_low), after_root % b_mid)
    b_window = b_root + b_own
    mine = jnp.where(block < b_root, block, b_root + within) + place * b_window
    theirs = 3 * b_window + place * b_own + within
    column_after = jnp.where((block < b_root) | (of == core), mine, theirs)
    t_mid = half(map_mid, core)[:, 0] - owner * local_blocks
    t_low = half(map_low, core)[:, 0] - owner * local_blocks
    first_mid = b_root + core * b_mid

    def forward(stack, right, *held):
        part = jnp.einsum("hnij,mnj->hnmi", stack, right, preferred_element_type=F32)
        width = part.size // owners // 8
        return scatter_sum(to_pieces(part.astype(BF16), owners, width), "subtree", *held)

    def whole(piece, shape, *held):
        got, *held = gather(piece.astype(BF16), "subtree", *held)
        return from_pieces(got, shape), *held

    def update_term(stack, y, *held):
        part = jnp.einsum("hnai,hnmi->nma", stack, y, preferred_element_type=F32)
        return full_sum(part, "z", *held)

    def placed(term, target, count):
        blocks = []
        for index in range(count):
            hit = (target == index)[:, None, None]
            blocks.append(jnp.sum(jnp.where(hit, term, 0.0), axis=0))
        return jnp.concatenate(blocks, axis=1)

    def back_term(stack, candidates, *held):
        g = jnp.zeros((stack.shape[1], modes, BLOCK), BF16)
        for hit, block in candidates:
            g = jnp.where(hit[:, None, None], block[None], g)
        part = jnp.einsum("hnai,nma->hnmi", stack, g, preferred_element_type=F32)
        width = part.size // owners // 8
        return scatter_sum(to_pieces(part.astype(BF16), owners, width), "subtree", *held)

    def transposed(stack, d, *held):
        part = jnp.einsum("hnij,hnmi->nmj", stack, d, preferred_element_type=F32)
        return full_sum(jnp.transpose(part, (1, 0, 2)).reshape(modes, -1), "z", *held)

    def cut(flat, target, count):
        return [(target == i, flat[:, i * BLOCK : (i + 1) * BLOCK]) for i in range(count)]

    stacked = side_by_side(modes_root, modes_mid, modes_low)
    before, after = neighbours(stacked)
    window = jnp.concatenate([before, stacked, after], axis=1)
    z_part = mass_partial(window, column, mass_vals).astype(BF16)

    def of_core(flat, which):
        mid = w_root + which * w_mid
        low = w_root + 2 * w_mid + which * 2 * w_low
        return jnp.concatenate(
            [flat[:, :w_root], flat[:, mid : mid + w_mid], flat[:, low : low + 2 * w_low]], axis=1
        )

    z_part = jnp.stack([of_core(z_part, 0), of_core(z_part, 1)]).reshape(
        2, layers, modes // layers, w_root + w_own
    )
    z_part = jnp.transpose(z_part, (1, 0, 2, 3)).reshape(2 * layers, *z_part.shape[2:])
    layer = lax.axis_index("z")
    t_own = t_low - first_mid
    z_part, t_mid, t_low, t_own, column_after, core, layer = lax.optimization_barrier(
        (z_part, t_mid, t_low, t_own, column_after, core, layer)
    )
    stacks, received = split_nodes(core, factor_low, factor_mid, update_low, update_mid)
    (z_mine,) = scatter_sum(z_part, FRONT)
    f_low, f_mid, u_low, u_mid = unpacked(stacks, received)
    (z,) = gather(z_mine.astype(BF16), "z")
    z = z.reshape(modes, -1)

    right = z[:, low_at:].reshape(modes, 2, w_low)
    y_low, t_low, t_own = forward(f_low, right, t_low, t_own)
    y, t_low, t_own = whole(y_low, (2, 2, modes, f_low.shape[-2]), t_low, t_own)
    term, t_low, t_own = update_term(u_low, y, t_low, t_own)
    acc_mid = placed(term, t_own, b_mid)
    acc_root = placed(term, t_low, b_root)
    right = (z[:, mid_at:low_at].astype(F32) - acc_mid).astype(BF16)
    right, acc_root = lax.optimization_barrier((right, acc_root))
    y_mid, t_mid = forward(f_mid, right.reshape(modes, 1, w_mid), t_mid)
    y, t_mid = whole(y_mid, (2, 1, modes, f_mid.shape[-2]), t_mid)
    term, t_mid, acc_root = update_term(u_mid, y, t_mid, acc_root)
    acc_root = acc_root + placed(term, t_mid, b_root)
    acc_root = acc_root + swap(acc_root)
    right = (z[:, :mid_at].astype(F32) - acc_root).astype(BF16)
    part = jnp.einsum("ij,mj->mi", factor_root[0], right, preferred_element_type=F32)
    (y_root,) = scatter_sum(to_pieces(part.astype(BF16), owners, 2 * BLOCK), "subtree")

    (d_root,) = whole(y_root, part.shape)
    part = jnp.einsum("ij,mi->mj", factor_root[0], d_root, preferred_element_type=F32)
    s_root, t_mid = full_sum(part + swap(part), "z", t_mid)
    x_root = s_root.astype(BF16)
    root_blocks = cut(x_root, t_mid, b_root)
    v_mid, y_mid, x_root = back_term(u_mid, root_blocks, y_mid, x_root)
    d_mid, x_root = whole(y_mid - v_mid, (2, 1, modes, f_mid.shape[-2]), x_root)
    s_mid, x_root, t_low, t_own = transposed(f_mid, d_mid, x_root, t_low, t_own)
    x_mid = s_mid.astype(BF16)
    blocks = cut(x_root, t_low, b_root) + cut(x_mid, t_own, b_mid)
    v_low, y_low, x_mid, x_root = back_term(u_low, blocks, y_low, x_mid, x_root)
    d_low, x_mid, x_root = whole(y_low - v_low, (2, 2, modes, f_low.shape[-2]), x_mid, x_root)
    s_low, x_mid, x_root, s_root, column_after, core, layer = transposed(
        f_low, d_low, x_mid, x_root, s_root, column_after, core, layer
    )
    x_low = s_low.astype(BF16)

    y_own = jnp.concatenate([x_root, x_mid, x_low], axis=1)
    before, after = neighbours(y_own)
    others = swap(jnp.concatenate([part[:, w_root:] for part in (before, y_own, after)], axis=1))
    window = jnp.concatenate([before, y_own, after, others], axis=1)
    my_part = mass_partial(window, column_after, mass_vals).astype(BF16)

    other = others[:, w_own : 2 * w_own]
    own = y_own[:, w_root:]
    first = jnp.where(core == 0, own, other)
    second = jnp.where(core == 0, other, own)
    y_all = jnp.concatenate(
        [x_root, first[:, :w_mid], second[:, :w_mid], first[:, w_mid:], second[:, w_mid:]], axis=1
    )

    mass_part = jnp.einsum("jr,kr->jk", y_all, my_part, preferred_element_type=F32)
    size = modes // layers
    y_mine = lax.dynamic_slice_in_dim(y_own, layer * size, size, axis=0)
    rows = lax.broadcasted_iota(jnp.int32, y_mine.shape, 1)
    y_mine = jnp.where((core == 0) | (rows >= w_root), y_mine, 0).astype(BF16)
    stiff_part = jnp.einsum("jr,kr->jk", y_mine, z, preferred_element_type=F32)

    def paired(value):
        size = value.shape[0] // 2
        return jnp.concatenate([value[:size], value[size:]], axis=1)

    n_mass, n_stiff = modes // 2, size // 2
    grams = jnp.concatenate([paired(mass_part), paired(stiff_part)], axis=0)
    grams = jnp.pad(grams, ((0, -(n_mass + n_stiff) % 8), (0, 0)))
    grams, y_all, s_root = full_sum(grams, "subtree", y_all, s_root)
    (grams,) = gather(grams.astype(BF16), FRONT)
    stiff, mass = unpaired(grams, n_mass, n_stiff)

    def output(flat, count):
        return jnp.transpose(flat.reshape(modes, count, -1), (1, 0, 2)).astype(F32)

    low_from = w_root + 2 * w_mid
    return (
        s_root[None],
        output(y_all[:, w_root:low_from], 2),
        output(y_all[:, low_from:], 4),
        stiff,
        mass,
    )


def solution(mesh):
    owners, fronts = mesh.shape["subtree"], mesh.shape["front"]
    split = Mesh(mesh.devices.reshape(owners, fronts // 2, 2), ("subtree", *FRONT))
    factor = P(None, FRONT, "subtree")
    update = P(None, "subtree", FRONT)
    rows = P(None, None, "subtree")

    return jax.shard_map(
        per_device,
        mesh=split,
        in_specs=(
            rows,
            rows,
            rows,
            factor,
            factor,
            factor,
            update,
            update,
            P(None, "subtree"),
            P(None, "subtree"),
            P("subtree", FRONT, None, None),
            P("subtree", FRONT),
        ),
        out_specs=(rows, rows, rows, P(), P()),
        check_vma=False,
    )
```

profile of v0, /device:TPU:1, one launch (start us, length us, event | category | flops | bytes accessed | tf_op | source)
XLA Modules:
  0.0 345.5 jit_solution(12052972551863341771)
XLA Ops:
  0.7 1.7 side_by_side.1
  2.4 1.3 collective-permute-start.1
  3.7 4.7 %collective-permute-start = (bf16[64,1920]{1,0:T(8,128)(2,1)}, bf16[64,1920]{1,0:T(8,128)(2,1)S(1)}, u32[]{:S(2)}, u32[]{:S(2)}) collective-permute-start(bf16[64,1920]{1,0:T(8,128)(2,1)} %side_by_side.1), channel_id=1, source_target_pairs={{0,16},{16,32},{32,48},{48,64},{64,80},{80,96},{96,112},{112,128},... | collective-permute-start | bytes 737288 | tf_op jit(solution)/shard_map/ppermute | solution.py:46
  8.3 0.7 fusion.67
  9.0 1.2 constant_dynamic-slice_fusion.1
  10.9 0.7 broadcast_subtract_fusion
  11.8 1.1 copy_bitcast_fusion.1
  12.9 0.6 gather_fusion
  14.2 3.0 pack.1
  17.2 9.2 %collective-permute-start.2 = (bf16[2304,256]{1,0:T(8,128)(2,1)}, bf16[2304,256]{1,0:T(8,128)(2,1)S(1)}, u32[]{:S(2)}, u32[]{:S(2)}) collective-permute-start(bf16[2304,256]{1,0:T(8,128)(2,1)} %get-tuple-element.71), channel_id=1, source_target_pairs={{0,1},{1,0},{2,3},{3,2},{4,5},{5,4},{6,7},{7,6},{8,9},{9,8},{10,11... | collective-permute-start | bytes 3538952 | tf_op jit(solution)/shard_map/ppermute | solution.py:41
  26.5 18.4 %all_to_all.95 = bf16[16,8,1152]{2,1,0:T(8,128)(2,1)S(1)} all-to-all(bf16[16,8,1152]{2,1,0:T(8,128)(2,1)S(1)} %bitcast.176), channel_id=1, replica_groups=mesh['subtree'=32,'z'=8,'core'=2] {'z','core'}, dimensions={0} | all-to-all | bytes 589824 | tf_op jit(solution)/shard_map/all_to_all | solution.py:22
  44.9 11.1 %all_to_all.96 = bf16[8,8,1152]{2,1,0:T(8,128)(2,1)S(1)} all-to-all(bf16[8,8,1152]{2,1,0:T(8,128)(2,1)S(1)} %broadcast_in_dim.269), channel_id=1, replica_groups=mesh['subtree'=32,'z'=8,'core'=2] {'z'}, dimensions={0} | all-to-all | bytes 294912 | tf_op jit(solution)/shard_map/all_to_all | solution.py:22
  56.0 0.6 copy-done.6
  56.7 1.1 unpack.1
  57.8 1.7 fusion
  59.5 21.3 %all_to_all.97 = bf16[32,8,512]{2,1,0:T(8,128)(2,1)S(1)} all-to-all(bf16[32,8,512]{2,1,0:T(8,128)(2,1)S(1)} %bitcast.178), channel_id=1, replica_groups=mesh['subtree'=32,'z'=8,'core'=2] {'subtree'}, dimensions={0} | all-to-all | bytes 524288 | tf_op jit(solution)/shard_map/all_to_all | solution.py:22
  80.8 14.8 %all_to_all.98 = bf16[32,8,512]{2,1,0:T(8,128)(2,1)S(1)} all-to-all(bf16[32,8,512]{2,1,0:T(8,128)(2,1)S(1)} %broadcast_in_dim.270), channel_id=1, replica_groups=mesh['subtree'=32,'z'=8,'core'=2] {'subtree'}, dimensions={0} | all-to-all | bytes 524288 | tf_op jit(solution)/shard_map/all_to_all | solution.py:22
  96.0 12.3 %all_to_all.99 = bf16[8,2,64,128]{3,2,1,0:T(8,128)(2,1)S(1)} all-to-all(bf16[8,2,64,128]{3,2,1,0:T(8,128)(2,1)S(1)} %broadcast_in_dim.271), channel_id=1, replica_groups=mesh['subtree'=32,'z'=8,'core'=2] {'z'}, dimensions={0} | all-to-all | bytes 524288 | tf_op jit(solution)/shard_map/all_to_all | solution.py:22
  108.8 14.8 %all_to_all.100 = bf16[32,8,256]{2,1,0:T(8,128)(2,1)S(1)} all-to-all(bf16[32,8,256]{2,1,0:T(8,128)(2,1)S(1)} %bitcast.186), channel_id=1, replica_groups=mesh['subtree'=32,'z'=8,'core'=2] {'subtree'}, dimensions={0} | all-to-all | bytes 262144 | tf_op jit(solution)/shard_map/all_to_all | solution.py:22
  123.7 12.6 %all_to_all.101 = bf16[32,8,256]{2,1,0:T(8,128)(2,1)S(1)} all-to-all(bf16[32,8,256]{2,1,0:T(8,128)(2,1)S(1)} %broadcast_in_dim.278), channel_id=1, replica_groups=mesh['subtree'=32,'z'=8,'core'=2] {'subtree'}, dimensions={0} | all-to-all | bytes 262144 | tf_op jit(solution)/shard_map/all_to_all | solution.py:22
  136.6 10.4 %all_to_all.102 = bf16[8,1,64,128]{3,2,1,0:T(8,128)(2,1)S(1)} all-to-all(bf16[8,1,64,128]{3,2,1,0:T(8,128)(2,1)S(1)} %broadcast_in_dim.279), channel_id=1, replica_groups=mesh['subtree'=32,'z'=8,'core'=2] {'z'}, dimensions={0} | all-to-all | bytes 262144 | tf_op jit(solution)/shard_map/all_to_all | solution.py:22
  147.0 9.2 %collective-permute-start.3 = (f32[64,384]{1,0:T(8,128)S(1)}, f32[64,384]{1,0:T(8,128)S(1)}, u32[]{:S(2)}, u32[]{:S(2)}) collective-permute-start(f32[64,384]{1,0:T(8,128)S(1)} %maximum_add_fusion), channel_id=1, source_target_pairs={{0,1},{1,0},{2,3},{3,2},{4,5},{5,4},{6,7},{7,6},{8,9},{9,8},{10,11... | collective-permute-start | bytes 294920 | tf_op jit(solution)/shard_map/ppermute | solution.py:41
  156.2 0.9 collective-permute-done.3
  157.5 12.4 %all_to_all.103 = bf16[32,8,256]{2,1,0:T(8,128)(2,1)S(1)} all-to-all(bf16[32,8,256]{2,1,0:T(8,128)(2,1)S(1)} %concatenate.58), channel_id=1, replica_groups=mesh['subtree'=32,'z'=8,'core'=2] {'subtree'}, dimensions={0} | all-to-all | bytes 262144 | tf_op jit(solution)/shard_map/all_to_all | solution.py:22
  170.0 13.3 %all_to_all.104 = bf16[32,8,256]{2,1,0:T(8,128)(2,1)S(1)} all-to-all(bf16[32,8,256]{2,1,0:T(8,128)(2,1)S(1)} %broadcast_in_dim.287), channel_id=1, replica_groups=mesh['subtree'=32,'z'=8,'core'=2] {'subtree'}, dimensions={0} | all-to-all | bytes 262144 | tf_op jit(solution)/shard_map/all_to_all | solution.py:22
  183.5 4.6 %collective-permute-start.4 = (f32[64,384]{1,0:T(8,128)S(1)}, f32[64,384]{1,0:T(8,128)S(1)}, u32[]{:S(2)}, u32[]{:S(2)}) collective-permute-start(f32[64,384]{1,0:T(8,128)S(1)} %fusion.10), channel_id=1, source_target_pairs={{0,1},{1,0},{2,3},{3,2},{4,5},{5,4},{6,7},{7,6},{8,9},{9,8},{10,11... | collective-permute-start | bytes 294920 | tf_op jit(solution)/shard_map/ppermute | solution.py:41
  188.2 0.9 collective-permute-done.4
  189.1 17.5 %all_to_all.105 = bf16[8,64,384]{2,1,0:T(8,128)(2,1)S(1)} all-to-all(bf16[8,64,384]{2,1,0:T(8,128)(2,1)S(1)} %broadcast_in_dim.288), channel_id=1, replica_groups=mesh['subtree'=32,'z'=8,'core'=2] {'z'}, dimensions={0} | all-to-all | bytes 786432 | tf_op jit(solution)/shard_map/all_to_all | solution.py:22
  206.9 12.3 %all_to_all.106 = bf16[32,8,256]{2,1,0:T(8,128)(2,1)S(1)} all-to-all(bf16[32,8,256]{2,1,0:T(8,128)(2,1)S(1)} %bitcast.183), channel_id=1, replica_groups=mesh['subtree'=32,'z'=8,'core'=2] {'subtree'}, dimensions={0} | all-to-all | bytes 262144 | tf_op jit(solution)/shard_map/all_to_all | solution.py:22
  219.4 13.2 %all_to_all.107 = bf16[32,8,256]{2,1,0:T(8,128)(2,1)S(1)} all-to-all(bf16[32,8,256]{2,1,0:T(8,128)(2,1)S(1)} %broadcast_in_dim.296), channel_id=1, replica_groups=mesh['subtree'=32,'z'=8,'core'=2] {'subtree'}, dimensions={0} | all-to-all | bytes 262144 | tf_op jit(solution)/shard_map/all_to_all | solution.py:22
  232.8 11.8 %all_to_all.108 = bf16[8,64,256]{2,1,0:T(8,128)(2,1)S(1)} all-to-all(bf16[8,64,256]{2,1,0:T(8,128)(2,1)S(1)} %broadcast_in_dim.297), channel_id=1, replica_groups=mesh['subtree'=32,'z'=8,'core'=2] {'z'}, dimensions={0} | all-to-all | bytes 524288 | tf_op jit(solution)/shard_map/all_to_all | solution.py:22
  245.0 13.6 %all_to_all.109 = bf16[32,8,512]{2,1,0:T(8,128)(2,1)S(1)} all-to-all(bf16[32,8,512]{2,1,0:T(8,128)(2,1)S(1)} %bitcast.179), channel_id=1, replica_groups=mesh['subtree'=32,'z'=8,'core'=2] {'subtree'}, dimensions={0} | all-to-all | bytes 524288 | tf_op jit(solution)/shard_map/all_to_all | solution.py:22
  258.6 14.0 %all_to_all.110 = bf16[32,8,512]{2,1,0:T(8,128)(2,1)S(1)} all-to-all(bf16[32,8,512]{2,1,0:T(8,128)(2,1)S(1)} %broadcast_in_dim.309), channel_id=1, replica_groups=mesh['subtree'=32,'z'=8,'core'=2] {'subtree'}, dimensions={0} | all-to-all | bytes 524288 | tf_op jit(solution)/shard_map/all_to_all | solution.py:22
  273.0 14.8 %all_to_all.111 = bf16[8,64,512]{2,1,0:T(8,128)(2,1)S(1)} all-to-all(bf16[8,64,512]{2,1,0:T(8,128)(2,1)S(1)} %broadcast_in_dim.310), channel_id=1, replica_groups=mesh['subtree'=32,'z'=8,'core'=2] {'z'}, dimensions={0} | all-to-all | bytes 1048576 | tf_op jit(solution)/shard_map/all_to_all | solution.py:22
  287.9 1.3 collective-permute-start.6
  289.2 4.3 %collective-permute-start.5 = (bf16[64,1152]{1,0:T(8,128)(2,1)S(1)}, bf16[64,1152]{1,0:T(8,128)(2,1)S(1)}, u32[]{:S(2)}, u32[]{:S(2)}) collective-permute-start(bf16[64,1152]{1,0:T(8,128)(2,1)S(1)} %pad_maximum_fusion.2), channel_id=1, source_target_pairs={{0,16},{16,32},{32,48},{48,64},{64,80},{80,96},{96,112},{112,128},... | collective-permute-start | bytes 442376 | tf_op jit(solution)/shard_map/ppermute | solution.py:46
  293.7 0.7 collective-permute-done.6
  294.4 1.2 collective-permute-done.5
  295.6 9.8 %collective-permute-start.7 = (bf16[64,2304]{1,0:T(8,128)(2,1)S(1)}, bf16[64,2304]{1,0:T(8,128)(2,1)S(1)}, u32[]{:S(2)}, u32[]{:S(2)}) collective-permute-start(bf16[64,2304]{1,0:T(8,128)(2,1)S(1)} %pad_maximum_fusion.1), channel_id=1, source_target_pairs={{0,1},{1,0},{2,3},{3,2},{4,5},{5,4},{6,7},{7,6},{8,9},{9,8},{10,11... | collective-permute-start | bytes 884744 | tf_op jit(solution)/shard_map/ppermute | solution.py:41
  305.6 1.1 collective-permute-done.7
  306.9 0.6 gather_fusion.1
  308.4 18.9 %all_to_all.112 = bf16[32,40,128]{2,1,0:T(8,128)(2,1)S(1)} all-to-all(bf16[32,40,128]{2,1,0:T(8,128)(2,1)S(1)} %broadcast_in_dim.313), channel_id=1, replica_groups=mesh['subtree'=32,'z'=8,'core'=2] {'subtree'}, dimensions={0} | all-to-all | bytes 655360 | tf_op jit(solution)/shard_map/all_to_all | solution.py:22
  327.4 0.7 broadcast_in_dim.315
  328.1 7.1 %all-to-all-start.18 = ((bf16[16,40,128]{2,1,0:T(8,128)(2,1)}), bf16[16,40,128]{2,1,0:T(8,128)(2,1)S(1)}, u32[]{:S(2)}, u32[]{:S(2)}) async-start(bf16[16,40,128]{2,1,0:T(8,128)(2,1)} %broadcast_in_dim.315), calls=%async_computation.18 | async-start | bytes 327680 | tf_op jit(solution)/shard_map/all_to_all | solution.py:22
  335.3 0.7 copy.55
  336.1 0.8 copy.56
  336.8 7.9 %all-to-all-done.18.grams = bf16[16,40,128]{2,1,0:T(8,128)(2,1)S(1)} async-done(((bf16[16,40,128]{2,1,0:T(8,128)(2,1)}), bf16[16,40,128]{2,1,0:T(8,128)(2,1)S(1)}, u32[]{:S(2)}, u32[]{:S(2)}) %all-to-all-start.18) | async-done | bytes 163872 | tf_op jit(solution)/shard_map/all_to_all | solution.py:22
  344.8 0.7 unpaired.1
  (116 shorter events, 5.7 us)
Async XLA Ops:
  0.6 156.5 %copy-start = (bf16[1,768,384]{2,1,0:T(8,128)(2,1)S(1)}, bf16[1,768,384]{2,1,0:T(8,128)(2,1)}, u32[]{:S(2)}) copy-start(bf16[1,768,384]{2,1,0:T(8,128)(2,1)} %param.15) | copy-start | bytes 1769476
  0.6 12.9 %copy-start.5 = (bf16[15,1,128,128]{3,2,1,0:T(8,128)(2,1)S(1)}, bf16[15,1,128,128]{3,2,1,0:T(8,128)(2,1)}, u32[]{:S(2)}) copy-start(bf16[15,1,128,128]{3,2,1,0:T(8,128)(2,1)} %param.22) | copy-start | bytes 1474564
  2.4 9.3 %collective-permute-start.1 = (bf16[64,1920]{1,0:T(8,128)(2,1)}, bf16[64,1920]{1,0:T(8,128)(2,1)S(1)}, u32[]{:S(2)}, u32[]{:S(2)}) collective-permute-start(bf16[64,1920]{1,0:T(8,128)(2,1)} %side_by_side.1), channel_id=1, source_target_pairs={{16,0},{32,16},{48,32},{64,48},{80,64},{96,80},{112,96},{128,112},... | collective-permute-start | bytes 737288 | tf_op jit(solution)/shard_map/ppermute | solution.py:47
  3.7 8.1 %collective-permute-start = (bf16[64,1920]{1,0:T(8,128)(2,1)}, bf16[64,1920]{1,0:T(8,128)(2,1)S(1)}, u32[]{:S(2)}, u32[]{:S(2)}) collective-permute-start(bf16[64,1920]{1,0:T(8,128)(2,1)} %side_by_side.1), channel_id=1, source_target_pairs={{0,16},{16,32},{32,48},{48,64},{64,80},{80,96},{96,112},{112,128},... | collective-permute-start | bytes 737288 | tf_op jit(solution)/shard_map/ppermute | solution.py:46
  17.2 39.5 %collective-permute-start.2 = (bf16[2304,256]{1,0:T(8,128)(2,1)}, bf16[2304,256]{1,0:T(8,128)(2,1)S(1)}, u32[]{:S(2)}, u32[]{:S(2)}) collective-permute-start(bf16[2304,256]{1,0:T(8,128)(2,1)} %get-tuple-element.71), channel_id=1, source_target_pairs={{0,1},{1,0},{2,3},{3,2},{4,5},{5,4},{6,7},{7,6},{8,9},{9,8},{10,11... | collective-permute-start | bytes 3538952 | tf_op jit(solution)/shard_map/ppermute | solution.py:41
  56.0 0.6 copy-start.6
  59.5 36.2 %copy-start.3 = (bf16[2,2,128,512]{3,2,1,0:T(8,128)(2,1)S(1)}, bf16[2,2,128,512]{3,2,1,0:T(8,128)(2,1)}, u32[]{:S(2)}) copy-start(bf16[2,2,128,512]{3,2,1,0:T(8,128)(2,1)} %get-tuple-element.83) | copy-start | bytes 1572868
  95.6 12.8 %copy-start.7 = (bf16[8,8,1152]{2,1,0:T(8,128)(2,1)S(1)}, bf16[8,8,1152]{2,1,0:T(8,128)(2,1)}, u32[]{:S(2)}) copy-start(bf16[8,8,1152]{2,1,0:T(8,128)(2,1)} %copy-done.6) | copy-start | bytes 442372
  95.6 12.9 %copy-start.2 = (bf16[2,1,512,256]{3,2,1,0:T(8,128)(2,1)S(1)}, bf16[2,1,512,256]{3,2,1,0:T(8,128)(2,1)}, u32[]{:S(2)}) copy-start(bf16[2,1,512,256]{3,2,1,0:T(8,128)(2,1)} %get-tuple-element.90) | copy-start | bytes 1572868
  108.3 28.0 %copy-start.4 = (bf16[2,1,128,512]{3,2,1,0:T(8,128)(2,1)S(1)}, bf16[2,1,128,512]{3,2,1,0:T(8,128)(2,1)}, u32[]{:S(2)}) copy-start(bf16[2,1,128,512]{3,2,1,0:T(8,128)(2,1)} %get-tuple-element.95) | copy-start | bytes 786436
  147.0 10.1 %collective-permute-start.3 = (f32[64,384]{1,0:T(8,128)S(1)}, f32[64,384]{1,0:T(8,128)S(1)}, u32[]{:S(2)}, u32[]{:S(2)}) collective-permute-start(f32[64,384]{1,0:T(8,128)S(1)} %maximum_add_fusion), channel_id=1, source_target_pairs={{0,1},{1,0},{2,3},{3,2},{4,5},{5,4},{6,7},{7,6},{8,9},{9,8},{10,11... | collective-permute-start | bytes 294920 | tf_op jit(solution)/shard_map/ppermute | solution.py:41
  183.5 5.5 %collective-permute-start.4 = (f32[64,384]{1,0:T(8,128)S(1)}, f32[64,384]{1,0:T(8,128)S(1)}, u32[]{:S(2)}, u32[]{:S(2)}) collective-permute-start(f32[64,384]{1,0:T(8,128)S(1)} %fusion.10), channel_id=1, source_target_pairs={{0,1},{1,0},{2,3},{3,2},{4,5},{5,4},{6,7},{7,6},{8,9},{9,8},{10,11... | collective-permute-start | bytes 294920 | tf_op jit(solution)/shard_map/ppermute | solution.py:41
  206.7 26.1 %copy-start.9 = (f32[64,384]{1,0:T(8,128)}, f32[64,384]{1,0:T(8,128)S(1)}, u32[]{:S(2)}) copy-start(f32[64,384]{1,0:T(8,128)S(1)} %convert_reduce_fusion) | copy-start | bytes 294916
  245.0 27.6 %copy-start.1 = (bf16[2,2,512,256]{3,2,1,0:T(8,128)(2,1)S(1)}, bf16[2,2,512,256]{3,2,1,0:T(8,128)(2,1)}, u32[]{:S(2)}) copy-start(bf16[2,2,512,256]{3,2,1,0:T(8,128)(2,1)} %get-tuple-element.76) | copy-start | bytes 3145732
  272.9 20.6 %copy-start.8 = (bf16[8,8,1152]{2,1,0:T(8,128)(2,1)S(1)}, bf16[8,8,1152]{2,1,0:T(8,128)(2,1)}, u32[]{:S(2)}) copy-start(bf16[8,8,1152]{2,1,0:T(8,128)(2,1)} %copy-done.6) | copy-start | bytes 442372
  287.9 6.5 %collective-permute-start.6 = (bf16[64,1152]{1,0:T(8,128)(2,1)S(1)}, bf16[64,1152]{1,0:T(8,128)(2,1)S(1)}, u32[]{:S(2)}, u32[]{:S(2)}) collective-permute-start(bf16[64,1152]{1,0:T(8,128)(2,1)S(1)} %pad_maximum_fusion.2), channel_id=1, source_target_pairs={{16,0},{32,16},{48,32},{64,48},{80,64},{96,80},{112,96},{128,112},... | collective-permute-start | bytes 442376 | tf_op jit(solution)/shard_map/ppermute | solution.py:47
  289.2 6.4 %collective-permute-start.5 = (bf16[64,1152]{1,0:T(8,128)(2,1)S(1)}, bf16[64,1152]{1,0:T(8,128)(2,1)S(1)}, u32[]{:S(2)}, u32[]{:S(2)}) collective-permute-start(bf16[64,1152]{1,0:T(8,128)(2,1)S(1)} %pad_maximum_fusion.2), channel_id=1, source_target_pairs={{0,16},{16,32},{32,48},{48,64},{64,80},{80,96},{96,112},{112,128},... | collective-permute-start | bytes 442376 | tf_op jit(solution)/shard_map/ppermute | solution.py:46
  295.6 11.0 %collective-permute-start.7 = (bf16[64,2304]{1,0:T(8,128)(2,1)S(1)}, bf16[64,2304]{1,0:T(8,128)(2,1)S(1)}, u32[]{:S(2)}, u32[]{:S(2)}) collective-permute-start(bf16[64,2304]{1,0:T(8,128)(2,1)S(1)} %pad_maximum_fusion.1), channel_id=1, source_target_pairs={{0,1},{1,0},{2,3},{3,2},{4,5},{5,4},{6,7},{7,6},{8,9},{9,8},{10,11... | collective-permute-start | bytes 884744 | tf_op jit(solution)/shard_map/ppermute | solution.py:41
  328.1 16.7 %all-to-all-start.18 = ((bf16[16,40,128]{2,1,0:T(8,128)(2,1)}), bf16[16,40,128]{2,1,0:T(8,128)(2,1)S(1)}, u32[]{:S(2)}, u32[]{:S(2)}) async-start(bf16[16,40,128]{2,1,0:T(8,128)(2,1)} %broadcast_in_dim.315), calls=%async_computation.18 | async-start | bytes 327680 | tf_op jit(solution)/shard_map/all_to_all | solution.py:22
where the time goes:
time: 347 us; the launch traced here: 346 us
  blocking collectives  258 us (74%)
  starting transfers between devices  51.5 us (15%)
  waiting for transfers between devices  12.8 us (4%)
  Pallas kernels  6.55 us (2%)
  local copies, waits for them, and re-layouts  6.24 us (2%)
  matrix products  5.18 us (1%)
  other arithmetic  3.63 us (1%)
    all_to_all x18, blocking collectives, exchange(): return lax.optimization_barrier((lax.all_to_all(pieces, axis, 0, 0), *held))  258 us
    ppermute x4, starting transfers between devices, swap(): return lax.ppermute(value, 'core', [(0, 1), (1, 0)])  32.9 us
    ppermute x2, starting transfers between devices, neighbours(): lax.ppermute(flat, 'subtree', [(i, i + 1) for i in range(count - 1)])  8.98 us
    all_to_all x1, waiting for transfers between devices, exchange(): return lax.optimization_barrier((lax.all_to_all(pieces, axis, 0, 0), *held))  7.94 us
    all_to_all x1, starting transfers between devices, exchange(): return lax.optimization_barrier((lax.all_to_all(pieces, axis, 0, 0), *held))  7.08 us
  transfers between devices with their start and end apart: 9, of which 7 were waited for; matrix products, arithmetic and copies ran while one was open for 1% of the time, Pallas kernels for 0%

commit v1 on v0

--- a/solution.py
+++ b/solution.py
@@ -284,6 +284,7 @@
 
     stacked = side_by_side(modes_root, modes_mid, modes_low)
     before, after = neighbours(stacked)
+    factors_root = (factor_root[0], swap(factor_root[0]))
     window = jnp.concatenate([before, stacked, after], axis=1)
     z_part = mass_partial(window, column, mass_vals).astype(BF16)
 
@@ -321,15 +322,35 @@
     y, t_mid = whole(y_mid, (2, 1, modes, f_mid.shape[-2]), t_mid)
     term, t_mid, acc_root = update_term(u_mid, y, t_mid, acc_root)
     acc_root = acc_root + placed(term, t_mid, b_root)
-    acc_root = acc_root + swap(acc_root)
-    right = (z[:, :mid_at].astype(F32) - acc_root).astype(BF16)
-    part = jnp.einsum("ij,mj->mi", factor_root[0], right, preferred_element_type=F32)
+
+    half_modes = modes // 2
+    z_root, t_mid, core = lax.optimization_barrier((z[:, :mid_at], t_mid, core))
+
+    def of_modes(value, which):
+        return lax.dynamic_slice_in_dim(value, which * half_modes, half_modes, 0)
+
+    acc_root = of_modes(acc_root, core) + swap(of_modes(acc_root, 1 - core))
+    right = (of_modes(z_root, core).astype(F32) - acc_root).astype(BF16)
+
+    def by_core(mine, other):
+        return jnp.concatenate(
+            [jnp.where(core == 0, mine, other), jnp.where(core == 0, other, mine)], axis=0
+        )
+
+    part = jnp.stack(
+        [jnp.einsum("ij,mj->mi", f, right, preferred_element_type=F32) for f in factors_root]
+    )
     (y_root,) = scatter_sum(to_pieces(part.astype(BF16), owners, 2 * BLOCK), "subtree")
 
-    (d_root,) = whole(y_root, part.shape)
-    part = jnp.einsum("ij,mi->mj", factor_root[0], d_root, preferred_element_type=F32)
-    s_root, t_mid = full_sum(part + swap(part), "z", t_mid)
-    x_root = s_root.astype(BF16)
+    d_root, t_mid, core = whole(y_root, part.shape, t_mid, core)
+    part = sum(
+        jnp.einsum("ij,mi->mj", f, d, preferred_element_type=F32)
+        for f, d in zip(factors_root, d_root)
+    )
+    s_half, t_mid, core = full_sum(part, "z", t_mid, core)
+    s_other = swap(s_half)
+    x_root = by_core(s_half.astype(BF16), s_other.astype(BF16))
+    x_root = lax.optimization_barrier(x_root)
     root_blocks = cut(x_root, t_mid, b_root)
     v_mid, y_mid, x_root = back_term(u_mid, root_blocks, y_mid, x_root)
     d_mid, x_root = whole(y_mid - v_mid, (2, 1, modes, f_mid.shape[-2]), x_root)
@@ -338,8 +359,8 @@
     blocks = cut(x_root, t_low, b_root) + cut(x_mid, t_own, b_mid)
     v_low, y_low, x_mid, x_root = back_term(u_low, blocks, y_low, x_mid, x_root)
     d_low, x_mid, x_root = whole(y_low - v_low, (2, 2, modes, f_low.shape[-2]), x_mid, x_root)
-    s_low, x_mid, x_root, s_root, column_after, core, layer = transposed(
-        f_low, d_low, x_mid, x_root, s_root, column_after, core, layer
+    s_low, x_mid, x_root, s_half, s_other, column_after, core, layer = transposed(
+        f_low, d_low, x_mid, x_root, s_half, s_other, column_after, core, layer
     )
     x_low = s_low.astype(BF16)
 
@@ -371,7 +392,7 @@
     n_mass, n_stiff = modes // 2, size // 2
     grams = jnp.concatenate([paired(mass_part), paired(stiff_part)], axis=0)
     grams = jnp.pad(grams, ((0, -(n_mass + n_stiff) % 8), (0, 0)))
-    grams, y_all, s_root = full_sum(grams, "subtree", y_all, s_root)
+    grams, y_all, s_half, s_other = full_sum(grams, "subtree", y_all, s_half, s_other)
     (grams,) = gather(grams.astype(BF16), FRONT)
     stiff, mass = unpaired(grams, n_mass, n_stiff)
 
@@ -379,13 +400,10 @@
         return jnp.transpose(flat.reshape(modes, count, -1), (1, 0, 2)).astype(F32)
 
     low_from = w_root + 2 * w_mid
-    return (
-        s_root[None],
-        output(y_all[:, w_root:low_from], 2),
-        output(y_all[:, low_from:], 4),
-        stiff,
-        mass,
-    )
+    solved_root = by_core(s_half, s_other)[None]
+    solved_mid = output(y_all[:, w_root:low_from], 2)
+    solved_low = output(y_all[:, low_from:], 4)
+    return solved_root, solved_mid, solved_low, stiff, mass
 
 
 def solution(mesh):

time: 347 us -> 345 us (level)
  blocking collectives: 258 us -> 239 us
  starting transfers between devices: 51.5 us -> 61.2 us
  waiting for transfers between devices: 12.8 us -> 18.6 us
    all_to_all x18 -> x17, blocking collectives: 258 us -> 239 us  [exchange(): return lax.optimization_barrier((lax.all_to_all(pieces, axis, 0, 0), *held))]
    ppermute x4 -> x5, starting transfers between devices: 32.9 us -> 40.6 us  [swap(): return lax.ppermute(value, 'core', [(0, 1), (1, 0)])]
    ppermute x2, waiting for transfers between devices: 0.66 us -> 6.25 us  [neighbours(): lax.ppermute(flat, 'subtree', [(i + 1, i) for i in range(count - 1)])]
    all_to_all x1 -> x2, starting transfers between devices: 7.08 us -> 10.5 us  [exchange(): return lax.optimization_barrier((lax.all_to_all(pieces, axis, 0, 0), *held))]
    all_to_all x1 -> x2, waiting for transfers between devices: 7.94 us -> 8.96 us  [exchange(): return lax.optimization_barrier((lax.all_to_all(pieces, axis, 0, 0), *held))]
  transfers between devices with their start and end apart: 9 -> 11, of which waited for: 7 -> 7; matrix products, arithmetic and copies ran while one was open for 1% -> 1% of each run, Pallas kernels for 0% -> 0%
where the time goes in v1:
time: 345 us; the launch traced here: 343 us
  blocking collectives  239 us (69%)
  starting transfers between devices  61.2 us (18%)
  waiting for transfers between devices  18.6 us (5%)
  Pallas kernels  6.51 us (2%)
  local copies, waits for them, and re-layouts  6.24 us (2%)
  matrix products  5.62 us (2%)
  other arithmetic  4.3 us (1%)
    all_to_all x17, blocking collectives, exchange(): return lax.optimization_barrier((lax.all_to_all(pieces, axis, 0, 0), *held))  239 us
    ppermute x5, starting transfers between devices, swap(): return lax.ppermute(value, 'core', [(0, 1), (1, 0)])  40.6 us
    all_to_all x2, starting transfers between devices, exchange(): return lax.optimization_barrier((lax.all_to_all(pieces, axis, 0, 0), *held))  10.5 us
    all_to_all x2, waiting for transfers between devices, exchange(): return lax.optimization_barrier((lax.all_to_all(pieces, axis, 0, 0), *held))  8.96 us
    ppermute x2, starting transfers between devices, neighbours(): lax.ppermute(flat, 'subtree', [(i, i + 1) for i in range(count - 1)])  7.64 us
  transfers between devices with their start and end apart: 11, of which 7 were waited for; matrix products, arithmetic and copies ran while one was open for 1% of the time, Pallas kernels for 0%

profile of v1, /device:TPU:1, one launch (start us, length us, event | category | flops | bytes accessed | tf_op | source)
XLA Modules:
  0.0 343.2 jit_solution(15106051548098778242)
XLA Ops:
  0.6 1.7 side_by_side.1
  2.3 4.0 %collective-permute-start = (bf16[64,1920]{1,0:T(8,128)(2,1)}, bf16[64,1920]{1,0:T(8,128)(2,1)S(1)}, u32[]{:S(2)}, u32[]{:S(2)}) collective-permute-start(bf16[64,1920]{1,0:T(8,128)(2,1)} %side_by_side.1), channel_id=1, source_target_pairs={{0,16},{16,32},{32,48},{48,64},{64,80},{80,96},{96,112},{112,128},... | collective-permute-start | bytes 737288 | tf_op jit(solution)/shard_map/ppermute | solution.py:46
  6.4 1.3 collective-permute-start.1
  7.7 0.7 fusion.66
  8.4 1.2 constant_dynamic-slice_fusion.2
  10.3 0.7 broadcast_subtract_fusion
  11.0 2.5 collective-permute-done.1
  13.5 1.1 copy_bitcast_fusion.1
  15.9 3.0 pack.1
  19.0 7.2 %collective-permute-start.2 = (bf16[2304,256]{1,0:T(8,128)(2,1)}, bf16[2304,256]{1,0:T(8,128)(2,1)S(1)}, u32[]{:S(2)}, u32[]{:S(2)}) collective-permute-start(bf16[2304,256]{1,0:T(8,128)(2,1)} %get-tuple-element.80), channel_id=1, source_target_pairs={{0,1},{1,0},{2,3},{3,2},{4,5},{5,4},{6,7},{7,6},{8,9},{9,8},{10,11... | collective-permute-start | bytes 3538952 | tf_op jit(solution)/shard_map/ppermute | solution.py:41
  26.2 20.6 %all_to_all.95 = bf16[16,8,1152]{2,1,0:T(8,128)(2,1)S(1)} all-to-all(bf16[16,8,1152]{2,1,0:T(8,128)(2,1)S(1)} %bitcast.187), channel_id=1, replica_groups=mesh['subtree'=32,'z'=8,'core'=2] {'z','core'}, dimensions={0} | all-to-all | bytes 589824 | tf_op jit(solution)/shard_map/all_to_all | solution.py:22
  46.8 11.1 %all_to_all.96 = bf16[8,8,1152]{2,1,0:T(8,128)(2,1)S(1)} all-to-all(bf16[8,8,1152]{2,1,0:T(8,128)(2,1)S(1)} %broadcast_in_dim.269), channel_id=1, replica_groups=mesh['subtree'=32,'z'=8,'core'=2] {'z'}, dimensions={0} | all-to-all | bytes 294912 | tf_op jit(solution)/shard_map/all_to_all | solution.py:22
  57.9 1.1 unpack.1
  59.0 1.7 fusion
  60.7 19.4 %all_to_all.97 = bf16[32,8,512]{2,1,0:T(8,128)(2,1)S(1)} all-to-all(bf16[32,8,512]{2,1,0:T(8,128)(2,1)S(1)} %bitcast.189), channel_id=1, replica_groups=mesh['subtree'=32,'z'=8,'core'=2] {'subtree'}, dimensions={0} | all-to-all | bytes 524288 | tf_op jit(solution)/shard_map/all_to_all | solution.py:22
  80.3 14.8 %all_to_all.98 = bf16[32,8,512]{2,1,0:T(8,128)(2,1)S(1)} all-to-all(bf16[32,8,512]{2,1,0:T(8,128)(2,1)S(1)} %broadcast_in_dim.270), channel_id=1, replica_groups=mesh['subtree'=32,'z'=8,'core'=2] {'subtree'}, dimensions={0} | all-to-all | bytes 524288 | tf_op jit(solution)/shard_map/all_to_all | solution.py:22
  95.4 12.3 %all_to_all.99 = bf16[8,2,64,128]{3,2,1,0:T(8,128)(2,1)S(1)} all-to-all(bf16[8,2,64,128]{3,2,1,0:T(8,128)(2,1)S(1)} %broadcast_in_dim.271), channel_id=1, replica_groups=mesh['subtree'=32,'z'=8,'core'=2] {'z'}, dimensions={0} | all-to-all | bytes 524288 | tf_op jit(solution)/shard_map/all_to_all | solution.py:22
  108.2 14.8 %all_to_all.100 = bf16[32,8,256]{2,1,0:T(8,128)(2,1)S(1)} all-to-all(bf16[32,8,256]{2,1,0:T(8,128)(2,1)S(1)} %bitcast.197), channel_id=1, replica_groups=mesh['subtree'=32,'z'=8,'core'=2] {'subtree'}, dimensions={0} | all-to-all | bytes 262144 | tf_op jit(solution)/shard_map/all_to_all | solution.py:22
  123.1 12.6 %all_to_all.101 = bf16[32,8,256]{2,1,0:T(8,128)(2,1)S(1)} all-to-all(bf16[32,8,256]{2,1,0:T(8,128)(2,1)S(1)} %broadcast_in_dim.278), channel_id=1, replica_groups=mesh['subtree'=32,'z'=8,'core'=2] {'subtree'}, dimensions={0} | all-to-all | bytes 262144 | tf_op jit(solution)/shard_map/all_to_all | solution.py:22
  135.9 0.7 broadcast_in_dim.279
  136.6 3.4 all-to-all-start.7
  140.0 8.1 %collective-permute-start.4 = (bf16[768,384]{1,0:T(8,128)(2,1)S(1)}, bf16[768,384]{1,0:T(8,128)(2,1)S(1)}, u32[]{:S(2)}, u32[]{:S(2)}) collective-permute-start(bf16[768,384]{1,0:T(8,128)(2,1)S(1)} %bitcast.179), channel_id=1, source_target_pairs={{0,1},{1,0},{2,3},{3,2},{4,5},{5,4},{6,7},{7,6},{8,9},{9,8},{10,11... | collective-permute-start | bytes 1769480 | tf_op jit(solution)/shard_map/ppermute | solution.py:41
  148.3 8.9 %collective-permute-start.3 = (f32[32,384]{1,0:T(8,128)S(1)}, f32[32,384]{1,0:T(8,128)S(1)}, u32[]{:S(2)}, u32[]{:S(2)}) collective-permute-start(f32[32,384]{1,0:T(8,128)S(1)} %constant_dynamic-slice_fusion), channel_id=1, source_target_pairs={{0,1},{1,0},{2,3},{3,2},{4,5},{5,4},{6,7},{7,6},{8,9},{9,8},{10,11... | collective-permute-start | bytes 147464 | tf_op jit(solution)/shard_map/ppermute | solution.py:41
  157.2 0.9 collective-permute-done.3
  158.7 12.4 %all_to_all.102 = bf16[32,8,256]{2,1,0:T(8,128)(2,1)S(1)} all-to-all(bf16[32,8,256]{2,1,0:T(8,128)(2,1)S(1)} %concatenate.64), channel_id=1, replica_groups=mesh['subtree'=32,'z'=8,'core'=2] {'subtree'}, dimensions={0} | all-to-all | bytes 262144 | tf_op jit(solution)/shard_map/all_to_all | solution.py:22
  171.2 13.3 %all_to_all.103 = bf16[32,8,256]{2,1,0:T(8,128)(2,1)S(1)} all-to-all(bf16[32,8,256]{2,1,0:T(8,128)(2,1)S(1)} %broadcast_in_dim.287), channel_id=1, replica_groups=mesh['subtree'=32,'z'=8,'core'=2] {'subtree'}, dimensions={0} | all-to-all | bytes 262144 | tf_op jit(solution)/shard_map/all_to_all | solution.py:22
  185.0 11.0 %all_to_all.104 = bf16[8,32,384]{2,1,0:T(8,128)(2,1)S(1)} all-to-all(bf16[8,32,384]{2,1,0:T(8,128)(2,1)S(1)} %broadcast_in_dim.288), channel_id=1, replica_groups=mesh['subtree'=32,'z'=8,'core'=2] {'z'}, dimensions={0} | all-to-all | bytes 393216 | tf_op jit(solution)/shard_map/all_to_all | solution.py:22
  196.1 5.8 %collective-permute-start.5 = (f32[32,384]{1,0:T(8,128)S(1)}, f32[32,384]{1,0:T(8,128)S(1)}, u32[]{:S(2)}, u32[]{:S(2)}) collective-permute-start(f32[32,384]{1,0:T(8,128)S(1)} %convert_reduce_fusion.3), channel_id=1, source_target_pairs={{0,1},{1,0},{2,3},{3,2},{4,5},{5,4},{6,7},{7,6},{8,9},{9,8},{10,11... | collective-permute-start | bytes 147464 | tf_op jit(solution)/shard_map/ppermute | solution.py:41
  201.9 0.8 collective-permute-done.5
  202.9 12.3 %all_to_all.105 = bf16[32,8,256]{2,1,0:T(8,128)(2,1)S(1)} all-to-all(bf16[32,8,256]{2,1,0:T(8,128)(2,1)S(1)} %bitcast.194), channel_id=1, replica_groups=mesh['subtree'=32,'z'=8,'core'=2] {'subtree'}, dimensions={0} | all-to-all | bytes 262144 | tf_op jit(solution)/shard_map/all_to_all | solution.py:22
  215.3 13.3 %all_to_all.106 = bf16[32,8,256]{2,1,0:T(8,128)(2,1)S(1)} all-to-all(bf16[32,8,256]{2,1,0:T(8,128)(2,1)S(1)} %broadcast_in_dim.296), channel_id=1, replica_groups=mesh['subtree'=32,'z'=8,'core'=2] {'subtree'}, dimensions={0} | all-to-all | bytes 262144 | tf_op jit(solution)/shard_map/all_to_all | solution.py:22
  228.9 11.8 %all_to_all.107 = bf16[8,64,256]{2,1,0:T(8,128)(2,1)S(1)} all-to-all(bf16[8,64,256]{2,1,0:T(8,128)(2,1)S(1)} %broadcast_in_dim.297), channel_id=1, replica_groups=mesh['subtree'=32,'z'=8,'core'=2] {'z'}, dimensions={0} | all-to-all | bytes 524288 | tf_op jit(solution)/shard_map/all_to_all | solution.py:22
  241.1 13.6 %all_to_all.108 = bf16[32,8,512]{2,1,0:T(8,128)(2,1)S(1)} all-to-all(bf16[32,8,512]{2,1,0:T(8,128)(2,1)S(1)} %bitcast.190), channel_id=1, replica_groups=mesh['subtree'=32,'z'=8,'core'=2] {'subtree'}, dimensions={0} | all-to-all | bytes 524288 | tf_op jit(solution)/shard_map/all_to_all | solution.py:22
  254.8 13.8 %all_to_all.109 = bf16[32,8,512]{2,1,0:T(8,128)(2,1)S(1)} all-to-all(bf16[32,8,512]{2,1,0:T(8,128)(2,1)S(1)} %broadcast_in_dim.309), channel_id=1, replica_groups=mesh['subtree'=32,'z'=8,'core'=2] {'subtree'}, dimensions={0} | all-to-all | bytes 524288 | tf_op jit(solution)/shard_map/all_to_all | solution.py:22
  268.9 14.7 %all_to_all.110 = bf16[8,64,512]{2,1,0:T(8,128)(2,1)S(1)} all-to-all(bf16[8,64,512]{2,1,0:T(8,128)(2,1)S(1)} %broadcast_in_dim.310), channel_id=1, replica_groups=mesh['subtree'=32,'z'=8,'core'=2] {'z'}, dimensions={0} | all-to-all | bytes 1048576 | tf_op jit(solution)/shard_map/all_to_all | solution.py:22
  283.7 3.6 %collective-permute-start.6 = (bf16[64,1152]{1,0:T(8,128)(2,1)S(1)}, bf16[64,1152]{1,0:T(8,128)(2,1)S(1)}, u32[]{:S(2)}, u32[]{:S(2)}) collective-permute-start(bf16[64,1152]{1,0:T(8,128)(2,1)S(1)} %pad_maximum_fusion.2), channel_id=1, source_target_pairs={{0,16},{16,32},{32,48},{48,64},{64,80},{80,96},{96,112},{112,128},... | collective-permute-start | bytes 442376 | tf_op jit(solution)/shard_map/ppermute | solution.py:46
  287.3 1.3 collective-permute-start.7
  289.4 3.7 %collective-permute-done.7 = bf16[64,1152]{1,0:T(8,128)(2,1)S(1)} collective-permute-done((bf16[64,1152]{1,0:T(8,128)(2,1)S(1)}, bf16[64,1152]{1,0:T(8,128)(2,1)S(1)}, u32[]{:S(2)}, u32[]{:S(2)}) %collective-permute-start.7) | collective-permute-done | bytes 147488 | tf_op jit(solution)/shard_map/ppermute | solution.py:47
  293.2 10.6 %collective-permute-start.8 = (bf16[64,2304]{1,0:T(8,128)(2,1)S(1)}, bf16[64,2304]{1,0:T(8,128)(2,1)S(1)}, u32[]{:S(2)}, u32[]{:S(2)}) collective-permute-start(bf16[64,2304]{1,0:T(8,128)(2,1)S(1)} %pad_maximum_fusion.1), channel_id=1, source_target_pairs={{0,1},{1,0},{2,3},{3,2},{4,5},{5,4},{6,7},{7,6},{8,9},{9,8},{10,11... | collective-permute-start | bytes 884744 | tf_op jit(solution)/shard_map/ppermute | solution.py:41
  303.8 1.1 collective-permute-done.8
  306.7 16.7 %all_to_all.111 = bf16[32,40,128]{2,1,0:T(8,128)(2,1)S(1)} all-to-all(bf16[32,40,128]{2,1,0:T(8,128)(2,1)S(1)} %broadcast_in_dim.313), channel_id=1, replica_groups=mesh['subtree'=32,'z'=8,'core'=2] {'subtree'}, dimensions={0} | all-to-all | bytes 655360 | tf_op jit(solution)/shard_map/all_to_all | solution.py:22
  323.6 0.8 copy.56
  324.4 0.7 copy.55
  325.1 0.7 broadcast_in_dim.315
  325.8 7.1 %all-to-all-start.18 = ((bf16[16,40,128]{2,1,0:T(8,128)(2,1)}), bf16[16,40,128]{2,1,0:T(8,128)(2,1)S(1)}, u32[]{:S(2)}, u32[]{:S(2)}) async-start(bf16[16,40,128]{2,1,0:T(8,128)(2,1)} %broadcast_in_dim.315), calls=%async_computation.18 | async-start | bytes 327680 | tf_op jit(solution)/shard_map/all_to_all | solution.py:22
  332.9 0.6 maximum_bitcast_fusion.3
  333.5 9.0 %all-to-all-done.18.grams = bf16[16,40,128]{2,1,0:T(8,128)(2,1)S(1)} async-done(((bf16[16,40,128]{2,1,0:T(8,128)(2,1)}), bf16[16,40,128]{2,1,0:T(8,128)(2,1)S(1)}, u32[]{:S(2)}, u32[]{:S(2)}) %all-to-all-start.18) | async-done | bytes 163872 | tf_op jit(solution)/shard_map/all_to_all | solution.py:22
  342.5 0.7 unpaired.1
  (120 shorter events, 7.9 us)
Async XLA Ops:
  0.6 14.6 %copy-start = (bf16[15,1,128,128]{3,2,1,0:T(8,128)(2,1)S(1)}, bf16[15,1,128,128]{3,2,1,0:T(8,128)(2,1)}, u32[]{:S(2)}) copy-start(bf16[15,1,128,128]{3,2,1,0:T(8,128)(2,1)} %param.22) | copy-start | bytes 1474564
  2.3 8.7 %collective-permute-start = (bf16[64,1920]{1,0:T(8,128)(2,1)}, bf16[64,1920]{1,0:T(8,128)(2,1)S(1)}, u32[]{:S(2)}, u32[]{:S(2)}) collective-permute-start(bf16[64,1920]{1,0:T(8,128)(2,1)} %side_by_side.1), channel_id=1, source_target_pairs={{0,16},{16,32},{32,48},{48,64},{64,80},{80,96},{96,112},{112,128},... | collective-permute-start | bytes 737288 | tf_op jit(solution)/shard_map/ppermute | solution.py:46
  6.4 7.2 %collective-permute-start.1 = (bf16[64,1920]{1,0:T(8,128)(2,1)}, bf16[64,1920]{1,0:T(8,128)(2,1)S(1)}, u32[]{:S(2)}, u32[]{:S(2)}) collective-permute-start(bf16[64,1920]{1,0:T(8,128)(2,1)} %side_by_side.1), channel_id=1, source_target_pairs={{16,0},{32,16},{48,32},{64,48},{80,64},{96,80},{112,96},{128,112},... | collective-permute-start | bytes 737288 | tf_op jit(solution)/shard_map/ppermute | solution.py:47
  19.0 39.0 %collective-permute-start.2 = (bf16[2304,256]{1,0:T(8,128)(2,1)}, bf16[2304,256]{1,0:T(8,128)(2,1)S(1)}, u32[]{:S(2)}, u32[]{:S(2)}) collective-permute-start(bf16[2304,256]{1,0:T(8,128)(2,1)} %get-tuple-element.80), channel_id=1, source_target_pairs={{0,1},{1,0},{2,3},{3,2},{4,5},{5,4},{6,7},{7,6},{8,9},{9,8},{10,11... | collective-permute-start | bytes 3538952 | tf_op jit(solution)/shard_map/ppermute | solution.py:41
  60.7 34.4 %copy-start.3 = (bf16[2,2,128,512]{3,2,1,0:T(8,128)(2,1)S(1)}, bf16[2,2,128,512]{3,2,1,0:T(8,128)(2,1)}, u32[]{:S(2)}) copy-start(bf16[2,2,128,512]{3,2,1,0:T(8,128)(2,1)} %get-tuple-element.92) | copy-start | bytes 1572868
  95.1 12.9 %copy-start.2 = (bf16[2,1,512,256]{3,2,1,0:T(8,128)(2,1)S(1)}, bf16[2,1,512,256]{3,2,1,0:T(8,128)(2,1)}, u32[]{:S(2)}) copy-start(bf16[2,1,512,256]{3,2,1,0:T(8,128)(2,1)} %get-tuple-element.99) | copy-start | bytes 1572868
  107.7 28.0 %copy-start.4 = (bf16[2,1,128,512]{3,2,1,0:T(8,128)(2,1)S(1)}, bf16[2,1,128,512]{3,2,1,0:T(8,128)(2,1)}, u32[]{:S(2)}) copy-start(bf16[2,1,128,512]{3,2,1,0:T(8,128)(2,1)} %get-tuple-element.104) | copy-start | bytes 786436
  107.9 32.1 %copy-start.5 = (bf16[1,768,384]{2,1,0:T(8,128)(2,1)S(1)}, bf16[1,768,384]{2,1,0:T(8,128)(2,1)}, u32[]{:S(2)}) copy-start(bf16[1,768,384]{2,1,0:T(8,128)(2,1)} %param.15) | copy-start | bytes 1769476
  136.6 11.5 %all-to-all-start.7 = ((bf16[8,1,64,128]{3,2,1,0:T(8,128)(2,1)}), bf16[8,1,64,128]{3,2,1,0:T(8,128)(2,1)S(1)}, u32[]{:S(2)}, u32[]{:S(2)}) async-start(bf16[8,1,64,128]{3,2,1,0:T(8,128)(2,1)} %broadcast_in_dim.279), calls=%async_computation.7 | async-start | bytes 262144 | tf_op jit(solution)/shard_map/all_to_all | solution.py:22
  140.0 18.4 %collective-permute-start.4 = (bf16[768,384]{1,0:T(8,128)(2,1)S(1)}, bf16[768,384]{1,0:T(8,128)(2,1)S(1)}, u32[]{:S(2)}, u32[]{:S(2)}) collective-permute-start(bf16[768,384]{1,0:T(8,128)(2,1)S(1)} %bitcast.179), channel_id=1, source_target_pairs={{0,1},{1,0},{2,3},{3,2},{4,5},{5,4},{6,7},{7,6},{8,9},{9,8},{10,11... | collective-permute-start | bytes 1769480 | tf_op jit(solution)/shard_map/ppermute | solution.py:41
  148.3 9.8 %collective-permute-start.3 = (f32[32,384]{1,0:T(8,128)S(1)}, f32[32,384]{1,0:T(8,128)S(1)}, u32[]{:S(2)}, u32[]{:S(2)}) collective-permute-start(f32[32,384]{1,0:T(8,128)S(1)} %constant_dynamic-slice_fusion), channel_id=1, source_target_pairs={{0,1},{1,0},{2,3},{3,2},{4,5},{5,4},{6,7},{7,6},{8,9},{9,8},{10,11... | collective-permute-start | bytes 147464 | tf_op jit(solution)/shard_map/ppermute | solution.py:41
  196.1 6.6 %collective-permute-start.5 = (f32[32,384]{1,0:T(8,128)S(1)}, f32[32,384]{1,0:T(8,128)S(1)}, u32[]{:S(2)}, u32[]{:S(2)}) collective-permute-start(f32[32,384]{1,0:T(8,128)S(1)} %convert_reduce_fusion.3), channel_id=1, source_target_pairs={{0,1},{1,0},{2,3},{3,2},{4,5},{5,4},{6,7},{7,6},{8,9},{9,8},{10,11... | collective-permute-start | bytes 147464 | tf_op jit(solution)/shard_map/ppermute | solution.py:41
  241.1 27.5 %copy-start.1 = (bf16[2,2,512,256]{3,2,1,0:T(8,128)(2,1)S(1)}, bf16[2,2,512,256]{3,2,1,0:T(8,128)(2,1)}, u32[]{:S(2)}) copy-start(bf16[2,2,512,256]{3,2,1,0:T(8,128)(2,1)} %get-tuple-element.85) | copy-start | bytes 3145732
  283.7 5.7 %collective-permute-start.6 = (bf16[64,1152]{1,0:T(8,128)(2,1)S(1)}, bf16[64,1152]{1,0:T(8,128)(2,1)S(1)}, u32[]{:S(2)}, u32[]{:S(2)}) collective-permute-start(bf16[64,1152]{1,0:T(8,128)(2,1)S(1)} %pad_maximum_fusion.2), channel_id=1, source_target_pairs={{0,16},{16,32},{32,48},{48,64},{64,80},{80,96},{96,112},{112,128},... | collective-permute-start | bytes 442376 | tf_op jit(solution)/shard_map/ppermute | solution.py:46
  287.3 5.9 %collective-permute-start.7 = (bf16[64,1152]{1,0:T(8,128)(2,1)S(1)}, bf16[64,1152]{1,0:T(8,128)(2,1)S(1)}, u32[]{:S(2)}, u32[]{:S(2)}) collective-permute-start(bf16[64,1152]{1,0:T(8,128)(2,1)S(1)} %pad_maximum_fusion.2), channel_id=1, source_target_pairs={{16,0},{32,16},{48,32},{64,48},{80,64},{96,80},{112,96},{128,112},... | collective-permute-start | bytes 442376 | tf_op jit(solution)/shard_map/ppermute | solution.py:47
  293.2 11.8 %collective-permute-start.8 = (bf16[64,2304]{1,0:T(8,128)(2,1)S(1)}, bf16[64,2304]{1,0:T(8,128)(2,1)S(1)}, u32[]{:S(2)}, u32[]{:S(2)}) collective-permute-start(bf16[64,2304]{1,0:T(8,128)(2,1)S(1)} %pad_maximum_fusion.1), channel_id=1, source_target_pairs={{0,1},{1,0},{2,3},{3,2},{4,5},{5,4},{6,7},{7,6},{8,9},{9,8},{10,11... | collective-permute-start | bytes 884744 | tf_op jit(solution)/shard_map/ppermute | solution.py:41
  325.8 16.7 %all-to-all-start.18 = ((bf16[16,40,128]{2,1,0:T(8,128)(2,1)}), bf16[16,40,128]{2,1,0:T(8,128)(2,1)S(1)}, u32[]{:S(2)}, u32[]{:S(2)}) async-start(bf16[16,40,128]{2,1,0:T(8,128)(2,1)} %broadcast_in_dim.315), calls=%async_computation.18 | async-start | bytes 327680 | tf_op jit(solution)/shard_map/all_to_all | solution.py:22

commit v2 on v1

--- a/solution.py
+++ b/solution.py
@@ -134,7 +134,7 @@
         ],
         name="pack",
     )(core.reshape(1), *weights)
-    return stacks, swap(sent)
+    return stacks, sent
 
 
 def unpacked(stacks, received):
@@ -225,7 +225,6 @@
     local_blocks = b_root + 2 * b_mid + 4 * b_low
     b_own = b_mid + 2 * b_low
     w_own = b_own * BLOCK
-    mid_at, low_at = w_root, w_root + w_mid
 
     def half(value, which, axis=0):
         size = value.shape[axis] // 2
@@ -283,8 +282,11 @@
         return [(target == i, flat[:, i * BLOCK : (i + 1) * BLOCK]) for i in range(count)]
 
     stacked = side_by_side(modes_root, modes_mid, modes_low)
-    before, after = neighbours(stacked)
-    factors_root = (factor_root[0], swap(factor_root[0]))
+    layer = lax.axis_index("z")
+    t_own = t_low - first_mid
+    before, after, t_mid, t_low, t_own, column_after, layer = lax.optimization_barrier(
+        (*neighbours(stacked), t_mid, t_low, t_own, column_after, layer)
+    )
     window = jnp.concatenate([before, stacked, after], axis=1)
     z_part = mass_partial(window, column, mass_vals).astype(BF16)
 
@@ -295,36 +297,55 @@
             [flat[:, :w_root], flat[:, mid : mid + w_mid], flat[:, low : low + 2 * w_low]], axis=1
         )
 
-    z_part = jnp.stack([of_core(z_part, 0), of_core(z_part, 1)]).reshape(
-        2, layers, modes // layers, w_root + w_own
-    )
-    z_part = jnp.transpose(z_part, (1, 0, 2, 3)).reshape(2 * layers, *z_part.shape[2:])
-    layer = lax.axis_index("z")
-    t_own = t_low - first_mid
-    z_part, t_mid, t_low, t_own, column_after, core, layer = lax.optimization_barrier(
-        (z_part, t_mid, t_low, t_own, column_after, core, layer)
-    )
-    stacks, received = split_nodes(core, factor_low, factor_mid, update_low, update_mid)
-    (z_mine,) = scatter_sum(z_part, FRONT)
+    parts = of_core(z_part, 0), of_core(z_part, 1)
+    own = jnp.where(core == 0, parts[0], parts[1])
+    z_part = own.astype(F32) + swap(jnp.where(core == 0, parts[1], parts[0])).astype(F32)
+    tiles = jnp.transpose(
+        z_part.astype(BF16).reshape(layers, modes // layers, b_root + b_own, BLOCK), (0, 2, 1, 3)
+    )
+    b_rest = b_root + b_mid
+    rest = tiles[:, :b_rest]
+    lower = tiles[:, b_rest:].reshape(1, -1, modes // layers, BLOCK)
+    n_lower = lower.shape[1]
+    pieces = jnp.concatenate([jnp.broadcast_to(lower, (layers, *lower.shape[1:])), rest], axis=1)
+
+    pieces, core = lax.optimization_barrier((pieces, core))
+    stacks, sent = split_nodes(core, factor_low, factor_mid, update_low, update_mid)
+    sent, root_sent = lax.optimization_barrier((sent, factor_root[0]))
+    received, root_received = lax.optimization_barrier((swap(sent), swap(root_sent)))
+    factors_root = (factor_root[0], root_received)
+    (z,) = scatter_sum(pieces, "z")
     f_low, f_mid, u_low, u_mid = unpacked(stacks, received)
-    (z,) = gather(z_mine.astype(BF16), "z")
-    z = z.reshape(modes, -1)
-
-    right = z[:, low_at:].reshape(modes, 2, w_low)
-    y_low, t_low, t_own = forward(f_low, right, t_low, t_own)
+
+    def from_tiles(value, lead):
+        across = value.shape[-3]
+        return jnp.transpose(value, (*range(lead), lead + 1, lead, lead + 2)).reshape(
+            -1, across * BLOCK
+        )
+
+    z = z.astype(BF16)
+    z_low = from_tiles(z[:n_lower].reshape(layers, -1, *z.shape[1:]), 1)
+    z_low, z_rest = lax.optimization_barrier((z_low, z[n_lower:]))
+
+    y_low, t_low, t_own = forward(f_low, z_low.reshape(modes, 2, w_low), t_low, t_own)
     y, t_low, t_own = whole(y_low, (2, 2, modes, f_low.shape[-2]), t_low, t_own)
-    term, t_low, t_own = update_term(u_low, y, t_low, t_own)
+    part = jnp.einsum("hnai,hnmi->nma", u_low, y, preferred_element_type=F32).astype(BF16)
+    tiles = jnp.concatenate([part.reshape(-1, *z_rest.shape[1:]), z_rest], axis=0)
+    got, t_low, t_own = gather(tiles, "z", t_low, t_own)
+    term = total(got[:, : -b_rest]).reshape(part.shape)
+    z_rest = from_tiles(got[:, -b_rest:], 1)
+    z_root, z_mid = z_rest[:, :w_root], z_rest[:, w_root:]
     acc_mid = placed(term, t_own, b_mid)
     acc_root = placed(term, t_low, b_root)
-    right = (z[:, mid_at:low_at].astype(F32) - acc_mid).astype(BF16)
-    right, acc_root = lax.optimization_barrier((right, acc_root))
+    right = (z_mid.astype(F32) - acc_mid).astype(BF16)
+    right, acc_root, z_root, z_mid = lax.optimization_barrier((right, acc_root, z_root, z_mid))
     y_mid, t_mid = forward(f_mid, right.reshape(modes, 1, w_mid), t_mid)
     y, t_mid = whole(y_mid, (2, 1, modes, f_mid.shape[-2]), t_mid)
     term, t_mid, acc_root = update_term(u_mid, y, t_mid, acc_root)
     acc_root = acc_root + placed(term, t_mid, b_root)
 
     half_modes = modes // 2
-    z_root, t_mid, core = lax.optimization_barrier((z[:, :mid_at], t_mid, core))
+    z_root, t_mid, core = lax.optimization_barrier((z_root, t_mid, core))
 
     def of_modes(value, which):
         return lax.dynamic_slice_in_dim(value, which * half_modes, half_modes, 0)
@@ -383,6 +404,7 @@
     y_mine = lax.dynamic_slice_in_dim(y_own, layer * size, size, axis=0)
     rows = lax.broadcasted_iota(jnp.int32, y_mine.shape, 1)
     y_mine = jnp.where((core == 0) | (rows >= w_root), y_mine, 0).astype(BF16)
+    z = jnp.concatenate([z_root, z_mid, z_low], axis=1)
     stiff_part = jnp.einsum("jr,kr->jk", y_mine, z, preferred_element_type=F32)
 
     def paired(value):

time: 345 us -> 349 us (1.012)
  waiting for transfers between devices: 18.6 us -> 37 us
  blocking collectives: 239 us -> 221 us
    all_to_all x2, waiting for transfers between devices: 8.96 us -> 26.3 us  [exchange(): return lax.optimization_barrier((lax.all_to_all(pieces, axis, 0, 0), *held))]
    all_to_all x17 -> x16, blocking collectives: 239 us -> 221 us  [exchange(): return lax.optimization_barrier((lax.all_to_all(pieces, axis, 0, 0), *held))]
    all_to_all x2, starting transfers between devices: 10.5 us -> 15.2 us  [exchange(): return lax.optimization_barrier((lax.all_to_all(pieces, axis, 0, 0), *held))]
    ppermute x5 -> x6, starting transfers between devices: 40.6 us -> 36 us  [swap(): return lax.ppermute(value, 'core', [(0, 1), (1, 0)])]
  transfers between devices with their start and end apart: 11 -> 12, of which waited for: 7 -> 9; matrix products, arithmetic and copies ran while one was open for 1% -> 1% of each run, Pallas kernels for 0% -> 0%
where the time goes in v2:
time: 349 us; the launch traced here: 347 us
  blocking collectives  221 us (63%)
  starting transfers between devices  61.4 us (18%)
  waiting for transfers between devices  37 us (11%)
  matrix products  7.76 us (2%)
  Pallas kernels  6.51 us (2%)
  local copies, waits for them, and re-layouts  5.7 us (2%)
  other arithmetic  5.25 us (2%)
    all_to_all x16, blocking collectives, exchange(): return lax.optimization_barrier((lax.all_to_all(pieces, axis, 0, 0), *held))  221 us
    ppermute x6, starting transfers between devices, swap(): return lax.ppermute(value, 'core', [(0, 1), (1, 0)])  36 us
    all_to_all x2, waiting for transfers between devices, exchange(): return lax.optimization_barrier((lax.all_to_all(pieces, axis, 0, 0), *held))  26.3 us
    all_to_all x2, starting transfers between devices, exchange(): return lax.optimization_barrier((lax.all_to_all(pieces, axis, 0, 0), *held))  15.2 us
    ppermute x2, starting transfers between devices, neighbours(): lax.ppermute(flat, 'subtree', [(i, i + 1) for i in range(count - 1)])  7.63 us
  transfers between devices with their start and end apart: 12, of which 9 were waited for; matrix products, arithmetic and copies ran while one was open for 1% of the time, Pallas kernels for 0%

profile of v2, /device:TPU:1, one launch (start us, length us, event | category | flops | bytes accessed | tf_op | source)
XLA Modules:
  0.0 347.3 jit_solution(16174256238930037124)
XLA Ops:
  0.6 1.7 side_by_side.1
  2.3 4.0 %collective-permute-start = (bf16[64,1920]{1,0:T(8,128)(2,1)}, bf16[64,1920]{1,0:T(8,128)(2,1)S(1)}, u32[]{:S(2)}, u32[]{:S(2)}) collective-permute-start(bf16[64,1920]{1,0:T(8,128)(2,1)} %side_by_side.1), channel_id=1, source_target_pairs={{0,16},{16,32},{32,48},{48,64},{64,80},{80,96},{96,112},{112,128},... | collective-permute-start | bytes 737288 | tf_op jit(solution)/shard_map/ppermute | solution.py:46
  6.4 1.3 collective-permute-start.1
  8.4 1.2 constant_dynamic-slice_fusion.2
  10.3 0.7 broadcast_subtract_fusion
  11.0 2.5 collective-permute-done.1
  13.5 1.1 copy_bitcast_fusion.1
  15.9 7.2 %collective-permute-start.2 = (bf16[64,1152]{1,0:T(8,128)(2,1)S(1)}, bf16[64,1152]{1,0:T(8,128)(2,1)S(1)}, u32[]{:S(2)}, u32[]{:S(2)}) collective-permute-start(bf16[64,1152]{1,0:T(8,128)(2,1)S(1)} %broadcast_select_fusion), channel_id=1, source_target_pairs={{0,1},{1,0},{2,3},{3,2},{4,5},{5,4},{6,7},{7,6},{8,9},{9,8},{10,11... | collective-permute-start | bytes 442376 | tf_op jit(solution)/shard_map/ppermute | solution.py:41
  23.1 1.0 collective-permute-done.2
  24.2 0.9 pad_maximum_fusion
  25.1 3.0 pack.1
  28.2 2.4 collective-permute-start.3
  30.6 8.1 %all-to-all-start = ((bf16[8,37,8,128]{3,2,1,0:T(8,128)(2,1)}), bf16[8,37,8,128]{3,2,1,0:T(8,128)(2,1)S(1)}, u32[]{:S(2)}, u32[]{:S(2)}) async-start(bf16[8,37,8,128]{3,2,1,0:T(8,128)(2,1)} %pad_maximum_fusion), calls=%async_computation | async-start | bytes 1212416 | tf_op jit(solution)/shard_map/all_to_all | solution.py:22
  38.7 2.3 collective-permute-start.4
  41.0 17.4 %all-to-all-done = bf16[8,37,8,128]{3,2,1,0:T(8,128)(2,1)S(1)} async-done(((bf16[8,37,8,128]{3,2,1,0:T(8,128)(2,1)}), bf16[8,37,8,128]{3,2,1,0:T(8,128)(2,1)S(1)}, u32[]{:S(2)}, u32[]{:S(2)}) %all-to-all-start) | async-done | bytes 606240 | tf_op jit(solution)/shard_map/all_to_all | solution.py:22
  58.6 1.1 unpack.1
  59.7 1.7 fusion
  61.4 19.5 %all_to_all.90 = bf16[32,8,512]{2,1,0:T(8,128)(2,1)S(1)} all-to-all(bf16[32,8,512]{2,1,0:T(8,128)(2,1)S(1)} %bitcast.203), channel_id=1, replica_groups=mesh['subtree'=32,'z'=8,'core'=2] {'subtree'}, dimensions={0} | all-to-all | bytes 524288 | tf_op jit(solution)/shard_map/all_to_all | solution.py:22
  80.9 15.9 %all_to_all.91 = bf16[32,8,512]{2,1,0:T(8,128)(2,1)S(1)} all-to-all(bf16[32,8,512]{2,1,0:T(8,128)(2,1)S(1)} %broadcast_in_dim.272), channel_id=1, replica_groups=mesh['subtree'=32,'z'=8,'core'=2] {'subtree'}, dimensions={0} | all-to-all | bytes 524288 | tf_op jit(solution)/shard_map/all_to_all | solution.py:22
  97.2 12.8 %all_to_all.92 = bf16[8,21,8,128]{3,2,1,0:T(8,128)(2,1)S(1)} all-to-all(bf16[8,21,8,128]{3,2,1,0:T(8,128)(2,1)S(1)} %broadcast_in_dim.273), channel_id=1, replica_groups=mesh['subtree'=32,'z'=8,'core'=2] {'z'}, dimensions={0} | all-to-all | bytes 688128 | tf_op jit(solution)/shard_map/all_to_all | solution.py:22
  110.6 16.8 %all_to_all.93 = bf16[32,8,256]{2,1,0:T(8,128)(2,1)S(1)} all-to-all(bf16[32,8,256]{2,1,0:T(8,128)(2,1)S(1)} %bitcast.211), channel_id=1, replica_groups=mesh['subtree'=32,'z'=8,'core'=2] {'subtree'}, dimensions={0} | all-to-all | bytes 262144 | tf_op jit(solution)/shard_map/all_to_all | solution.py:22
  127.4 12.6 %all_to_all.94 = bf16[32,8,256]{2,1,0:T(8,128)(2,1)S(1)} all-to-all(bf16[32,8,256]{2,1,0:T(8,128)(2,1)S(1)} %broadcast_in_dim.280), channel_id=1, replica_groups=mesh['subtree'=32,'z'=8,'core'=2] {'subtree'}, dimensions={0} | all-to-all | bytes 262144 | tf_op jit(solution)/shard_map/all_to_all | solution.py:22
  140.3 11.0 %all_to_all.95 = bf16[8,1,64,128]{3,2,1,0:T(8,128)(2,1)S(1)} all-to-all(bf16[8,1,64,128]{3,2,1,0:T(8,128)(2,1)S(1)} %broadcast_in_dim.281), channel_id=1, replica_groups=mesh['subtree'=32,'z'=8,'core'=2] {'z'}, dimensions={0} | all-to-all | bytes 262144 | tf_op jit(solution)/shard_map/all_to_all | solution.py:22
  151.4 7.7 %collective-permute-start.5 = (f32[32,384]{1,0:T(8,128)S(1)}, f32[32,384]{1,0:T(8,128)S(1)}, u32[]{:S(2)}, u32[]{:S(2)}) collective-permute-start(f32[32,384]{1,0:T(8,128)S(1)} %constant_dynamic-slice_fusion), channel_id=1, source_target_pairs={{0,1},{1,0},{2,3},{3,2},{4,5},{5,4},{6,7},{7,6},{8,9},{9,8},{10,11... | collective-permute-start | bytes 147464 | tf_op jit(solution)/shard_map/ppermute | solution.py:41
  159.1 0.9 collective-permute-done.5
  160.3 1.4 fusion.9
  161.7 12.4 %all_to_all.96 = bf16[32,8,256]{2,1,0:T(8,128)(2,1)S(1)} all-to-all(bf16[32,8,256]{2,1,0:T(8,128)(2,1)S(1)} %concatenate.74), channel_id=1, replica_groups=mesh['subtree'=32,'z'=8,'core'=2] {'subtree'}, dimensions={0} | all-to-all | bytes 262144 | tf_op jit(solution)/shard_map/all_to_all | solution.py:22
  174.2 13.3 %all_to_all.97 = bf16[32,8,256]{2,1,0:T(8,128)(2,1)S(1)} all-to-all(bf16[32,8,256]{2,1,0:T(8,128)(2,1)S(1)} %broadcast_in_dim.289), channel_id=1, replica_groups=mesh['subtree'=32,'z'=8,'core'=2] {'subtree'}, dimensions={0} | all-to-all | bytes 262144 | tf_op jit(solution)/shard_map/all_to_all | solution.py:22
  187.8 1.3 fusion.10
  189.1 11.0 %all_to_all.98 = bf16[8,32,384]{2,1,0:T(8,128)(2,1)S(1)} all-to-all(bf16[8,32,384]{2,1,0:T(8,128)(2,1)S(1)} %broadcast_in_dim.290), channel_id=1, replica_groups=mesh['subtree'=32,'z'=8,'core'=2] {'z'}, dimensions={0} | all-to-all | bytes 393216 | tf_op jit(solution)/shard_map/all_to_all | solution.py:22
  200.1 5.8 %collective-permute-start.6 = (f32[32,384]{1,0:T(8,128)S(1)}, f32[32,384]{1,0:T(8,128)S(1)}, u32[]{:S(2)}, u32[]{:S(2)}) collective-permute-start(f32[32,384]{1,0:T(8,128)S(1)} %convert_reduce_fusion.3), channel_id=1, source_target_pairs={{0,1},{1,0},{2,3},{3,2},{4,5},{5,4},{6,7},{7,6},{8,9},{9,8},{10,11... | collective-permute-start | bytes 147464 | tf_op jit(solution)/shard_map/ppermute | solution.py:41
  205.9 0.8 collective-permute-done.6
  207.0 12.3 %all_to_all.99 = bf16[32,8,256]{2,1,0:T(8,128)(2,1)S(1)} all-to-all(bf16[32,8,256]{2,1,0:T(8,128)(2,1)S(1)} %bitcast.208), channel_id=1, replica_groups=mesh['subtree'=32,'z'=8,'core'=2] {'subtree'}, dimensions={0} | all-to-all | bytes 262144 | tf_op jit(solution)/shard_map/all_to_all | solution.py:22
  219.4 13.3 %all_to_all.100 = bf16[32,8,256]{2,1,0:T(8,128)(2,1)S(1)} all-to-all(bf16[32,8,256]{2,1,0:T(8,128)(2,1)S(1)} %broadcast_in_dim.298), channel_id=1, replica_groups=mesh['subtree'=32,'z'=8,'core'=2] {'subtree'}, dimensions={0} | all-to-all | bytes 262144 | tf_op jit(solution)/shard_map/all_to_all | solution.py:22
  233.0 11.8 %all_to_all.101 = bf16[8,64,256]{2,1,0:T(8,128)(2,1)S(1)} all-to-all(bf16[8,64,256]{2,1,0:T(8,128)(2,1)S(1)} %broadcast_in_dim.299), channel_id=1, replica_groups=mesh['subtree'=32,'z'=8,'core'=2] {'z'}, dimensions={0} | all-to-all | bytes 524288 | tf_op jit(solution)/shard_map/all_to_all | solution.py:22
  245.2 13.6 %all_to_all.102 = bf16[32,8,512]{2,1,0:T(8,128)(2,1)S(1)} all-to-all(bf16[32,8,512]{2,1,0:T(8,128)(2,1)S(1)} %bitcast.204), channel_id=1, replica_groups=mesh['subtree'=32,'z'=8,'core'=2] {'subtree'}, dimensions={0} | all-to-all | bytes 524288 | tf_op jit(solution)/shard_map/all_to_all | solution.py:22
  258.8 13.8 %all_to_all.103 = bf16[32,8,512]{2,1,0:T(8,128)(2,1)S(1)} all-to-all(bf16[32,8,512]{2,1,0:T(8,128)(2,1)S(1)} %broadcast_in_dim.311), channel_id=1, replica_groups=mesh['subtree'=32,'z'=8,'core'=2] {'subtree'}, dimensions={0} | all-to-all | bytes 524288 | tf_op jit(solution)/shard_map/all_to_all | solution.py:22
  273.0 14.7 %all_to_all.104 = bf16[8,64,512]{2,1,0:T(8,128)(2,1)S(1)} all-to-all(bf16[8,64,512]{2,1,0:T(8,128)(2,1)S(1)} %broadcast_in_dim.312), channel_id=1, replica_groups=mesh['subtree'=32,'z'=8,'core'=2] {'z'}, dimensions={0} | all-to-all | bytes 1048576 | tf_op jit(solution)/shard_map/all_to_all | solution.py:22
  287.7 3.6 %collective-permute-start.7 = (bf16[64,1152]{1,0:T(8,128)(2,1)S(1)}, bf16[64,1152]{1,0:T(8,128)(2,1)S(1)}, u32[]{:S(2)}, u32[]{:S(2)}) collective-permute-start(bf16[64,1152]{1,0:T(8,128)(2,1)S(1)} %pad_maximum_fusion.4), channel_id=1, source_target_pairs={{0,16},{16,32},{32,48},{48,64},{64,80},{80,96},{96,112},{112,128},... | collective-permute-start | bytes 442376 | tf_op jit(solution)/shard_map/ppermute | solution.py:46
  291.3 1.3 collective-permute-start.8
  293.5 3.8 %collective-permute-done.8 = bf16[64,1152]{1,0:T(8,128)(2,1)S(1)} collective-permute-done((bf16[64,1152]{1,0:T(8,128)(2,1)S(1)}, bf16[64,1152]{1,0:T(8,128)(2,1)S(1)}, u32[]{:S(2)}, u32[]{:S(2)}) %collective-permute-start.8) | collective-permute-done | bytes 147488 | tf_op jit(solution)/shard_map/ppermute | solution.py:47
  297.3 10.6 %collective-permute-start.9 = (bf16[64,2304]{1,0:T(8,128)(2,1)S(1)}, bf16[64,2304]{1,0:T(8,128)(2,1)S(1)}, u32[]{:S(2)}, u32[]{:S(2)}) collective-permute-start(bf16[64,2304]{1,0:T(8,128)(2,1)S(1)} %pad_maximum_fusion.1), channel_id=1, source_target_pairs={{0,1},{1,0},{2,3},{3,2},{4,5},{5,4},{6,7},{7,6},{8,9},{9,8},{10,11... | collective-permute-start | bytes 884744 | tf_op jit(solution)/shard_map/ppermute | solution.py:41
  307.9 1.1 collective-permute-done.9
  310.8 16.7 %all_to_all.105 = bf16[32,40,128]{2,1,0:T(8,128)(2,1)S(1)} all-to-all(bf16[32,40,128]{2,1,0:T(8,128)(2,1)S(1)} %broadcast_in_dim.315), channel_id=1, replica_groups=mesh['subtree'=32,'z'=8,'core'=2] {'subtree'}, dimensions={0} | all-to-all | bytes 655360 | tf_op jit(solution)/shard_map/all_to_all | solution.py:22
  328.4 0.8 copy.52
  329.9 7.1 %all-to-all-start.17 = ((bf16[16,40,128]{2,1,0:T(8,128)(2,1)}), bf16[16,40,128]{2,1,0:T(8,128)(2,1)S(1)}, u32[]{:S(2)}, u32[]{:S(2)}) async-start(bf16[16,40,128]{2,1,0:T(8,128)(2,1)} %broadcast_in_dim.317), calls=%async_computation.17 | async-start | bytes 327680 | tf_op jit(solution)/shard_map/all_to_all | solution.py:22
  337.6 9.0 %all-to-all-done.17.grams = bf16[16,40,128]{2,1,0:T(8,128)(2,1)S(1)} async-done(((bf16[16,40,128]{2,1,0:T(8,128)(2,1)}), bf16[16,40,128]{2,1,0:T(8,128)(2,1)S(1)}, u32[]{:S(2)}, u32[]{:S(2)}) %all-to-all-start.17) | async-done | bytes 163872 | tf_op jit(solution)/shard_map/all_to_all | solution.py:22
  346.6 0.7 unpaired.1
  (133 shorter events, 10.2 us)
Async XLA Ops:
  0.6 14.6 %copy-start = (bf16[15,1,128,128]{3,2,1,0:T(8,128)(2,1)S(1)}, bf16[15,1,128,128]{3,2,1,0:T(8,128)(2,1)}, u32[]{:S(2)}) copy-start(bf16[15,1,128,128]{3,2,1,0:T(8,128)(2,1)} %param.22) | copy-start | bytes 1474564
  2.3 8.7 %collective-permute-start = (bf16[64,1920]{1,0:T(8,128)(2,1)}, bf16[64,1920]{1,0:T(8,128)(2,1)S(1)}, u32[]{:S(2)}, u32[]{:S(2)}) collective-permute-start(bf16[64,1920]{1,0:T(8,128)(2,1)} %side_by_side.1), channel_id=1, source_target_pairs={{0,16},{16,32},{32,48},{48,64},{64,80},{80,96},{96,112},{112,128},... | collective-permute-start | bytes 737288 | tf_op jit(solution)/shard_map/ppermute | solution.py:46
  6.4 7.2 %collective-permute-start.1 = (bf16[64,1920]{1,0:T(8,128)(2,1)}, bf16[64,1920]{1,0:T(8,128)(2,1)S(1)}, u32[]{:S(2)}, u32[]{:S(2)}) collective-permute-start(bf16[64,1920]{1,0:T(8,128)(2,1)} %side_by_side.1), channel_id=1, source_target_pairs={{16,0},{32,16},{48,32},{64,48},{80,64},{96,80},{112,96},{128,112},... | collective-permute-start | bytes 737288 | tf_op jit(solution)/shard_map/ppermute | solution.py:47
  15.9 8.2 %collective-permute-start.2 = (bf16[64,1152]{1,0:T(8,128)(2,1)S(1)}, bf16[64,1152]{1,0:T(8,128)(2,1)S(1)}, u32[]{:S(2)}, u32[]{:S(2)}) collective-permute-start(bf16[64,1152]{1,0:T(8,128)(2,1)S(1)} %broadcast_select_fusion), channel_id=1, source_target_pairs={{0,1},{1,0},{2,3},{3,2},{4,5},{5,4},{6,7},{7,6},{8,9},{9,8},{10,11... | collective-permute-start | bytes 442376 | tf_op jit(solution)/shard_map/ppermute | solution.py:41
  28.2 10.5 %copy-start.5 = (bf16[1,768,384]{2,1,0:T(8,128)(2,1)S(1)}, bf16[1,768,384]{2,1,0:T(8,128)(2,1)}, u32[]{:S(2)}) copy-start(bf16[1,768,384]{2,1,0:T(8,128)(2,1)} %param.15) | copy-start | bytes 1769476
  28.2 30.4 %collective-permute-start.3 = (bf16[2304,256]{1,0:T(8,128)(2,1)}, bf16[2304,256]{1,0:T(8,128)(2,1)S(1)}, u32[]{:S(2)}, u32[]{:S(2)}) collective-permute-start(bf16[2304,256]{1,0:T(8,128)(2,1)} %get-tuple-element.94), channel_id=1, source_target_pairs={{0,1},{1,0},{2,3},{3,2},{4,5},{5,4},{6,7},{7,6},{8,9},{9,8},{10,11... | collective-permute-start | bytes 3538952 | tf_op jit(solution)/shard_map/ppermute | solution.py:41
  30.6 27.8 %all-to-all-start = ((bf16[8,37,8,128]{3,2,1,0:T(8,128)(2,1)}), bf16[8,37,8,128]{3,2,1,0:T(8,128)(2,1)S(1)}, u32[]{:S(2)}, u32[]{:S(2)}) async-start(bf16[8,37,8,128]{3,2,1,0:T(8,128)(2,1)} %pad_maximum_fusion), calls=%async_computation | async-start | bytes 1212416 | tf_op jit(solution)/shard_map/all_to_all | solution.py:22
  38.7 19.9 %collective-permute-start.4 = (bf16[768,384]{1,0:T(8,128)(2,1)S(1)}, bf16[768,384]{1,0:T(8,128)(2,1)}, u32[]{:S(2)}, u32[]{:S(2)}) collective-permute-start(bf16[768,384]{1,0:T(8,128)(2,1)S(1)} %bitcast.197), channel_id=1, source_target_pairs={{0,1},{1,0},{2,3},{3,2},{4,5},{5,4},{6,7},{7,6},{8,9},{9,8},{10,11... | collective-permute-start | bytes 1769480 | tf_op jit(solution)/shard_map/ppermute | solution.py:41
  58.5 1.2 copy-start.7
  61.3 35.5 %copy-start.3 = (bf16[2,2,128,512]{3,2,1,0:T(8,128)(2,1)S(1)}, bf16[2,2,128,512]{3,2,1,0:T(8,128)(2,1)}, u32[]{:S(2)}) copy-start(bf16[2,2,128,512]{3,2,1,0:T(8,128)(2,1)} %get-tuple-element.108) | copy-start | bytes 1572868
  61.4 35.8 %slice-start.1 = ((bf16[37,8,128]{2,1,0:T(8,128)(2,1)}), bf16[5,8,128]{2,1,0:T(8,128)(2,1)S(1)}, s32[]{:S(2)}) async-start(bf16[37,8,128]{2,1,0:T(8,128)(2,1)} %copy-done.7), calls=%async_computation.19 | async-start | bytes 20480 | tf_op jit(solution)/shard_map/slice | solution.py:328
  97.2 13.1 %copy-start.2 = (bf16[2,1,512,256]{3,2,1,0:T(8,128)(2,1)S(1)}, bf16[2,1,512,256]{3,2,1,0:T(8,128)(2,1)}, u32[]{:S(2)}) copy-start(bf16[2,1,512,256]{3,2,1,0:T(8,128)(2,1)} %get-tuple-element.117) | copy-start | bytes 1572868
  110.1 29.9 %copy-start.4 = (bf16[2,1,128,512]{3,2,1,0:T(8,128)(2,1)S(1)}, bf16[2,1,128,512]{3,2,1,0:T(8,128)(2,1)}, u32[]{:S(2)}) copy-start(bf16[2,1,128,512]{3,2,1,0:T(8,128)(2,1)} %get-tuple-element.122) | copy-start | bytes 786436
  110.1 30.1 %copy-start.6 = (bf16[64,640]{1,0:T(8,128)(2,1)}, bf16[64,640]{1,0:T(8,128)(2,1)S(1)}, u32[]{:S(2)}) copy-start(bf16[64,640]{1,0:T(8,128)(2,1)S(1)} %slice_bitcast_fusion) | copy-start | bytes 245764
  151.4 8.6 %collective-permute-start.5 = (f32[32,384]{1,0:T(8,128)S(1)}, f32[32,384]{1,0:T(8,128)S(1)}, u32[]{:S(2)}, u32[]{:S(2)}) collective-permute-start(f32[32,384]{1,0:T(8,128)S(1)} %constant_dynamic-slice_fusion), channel_id=1, source_target_pairs={{0,1},{1,0},{2,3},{3,2},{4,5},{5,4},{6,7},{7,6},{8,9},{9,8},{10,11... | collective-permute-start | bytes 147464 | tf_op jit(solution)/shard_map/ppermute | solution.py:41
  200.1 6.6 %collective-permute-start.6 = (f32[32,384]{1,0:T(8,128)S(1)}, f32[32,384]{1,0:T(8,128)S(1)}, u32[]{:S(2)}, u32[]{:S(2)}) collective-permute-start(f32[32,384]{1,0:T(8,128)S(1)} %convert_reduce_fusion.3), channel_id=1, source_target_pairs={{0,1},{1,0},{2,3},{3,2},{4,5},{5,4},{6,7},{7,6},{8,9},{9,8},{10,11... | collective-permute-start | bytes 147464 | tf_op jit(solution)/shard_map/ppermute | solution.py:41
  245.1 27.5 %copy-start.1 = (bf16[2,2,512,256]{3,2,1,0:T(8,128)(2,1)S(1)}, bf16[2,2,512,256]{3,2,1,0:T(8,128)(2,1)}, u32[]{:S(2)}) copy-start(bf16[2,2,512,256]{3,2,1,0:T(8,128)(2,1)} %get-tuple-element.101) | copy-start | bytes 3145732
  272.9 19.7 %slice-start = ((bf16[64,640]{1,0:T(8,128)(2,1)}), bf16[64,256]{1,0:T(8,128)(2,1)S(1)}, s32[]{:S(2)}) async-start(bf16[64,640]{1,0:T(8,128)(2,1)} %copy-done.6), calls=%async_computation.18 | async-start | bytes 65536 | tf_op jit(solution)/shard_map/slice | solution.py:337
  287.7 5.7 %collective-permute-start.7 = (bf16[64,1152]{1,0:T(8,128)(2,1)S(1)}, bf16[64,1152]{1,0:T(8,128)(2,1)S(1)}, u32[]{:S(2)}, u32[]{:S(2)}) collective-permute-start(bf16[64,1152]{1,0:T(8,128)(2,1)S(1)} %pad_maximum_fusion.4), channel_id=1, source_target_pairs={{0,16},{16,32},{32,48},{48,64},{64,80},{80,96},{96,112},{112,128},... | collective-permute-start | bytes 442376 | tf_op jit(solution)/shard_map/ppermute | solution.py:46
  291.3 5.9 %collective-permute-start.8 = (bf16[64,1152]{1,0:T(8,128)(2,1)S(1)}, bf16[64,1152]{1,0:T(8,128)(2,1)S(1)}, u32[]{:S(2)}, u32[]{:S(2)}) collective-permute-start(bf16[64,1152]{1,0:T(8,128)(2,1)S(1)} %pad_maximum_fusion.4), channel_id=1, source_target_pairs={{16,0},{32,16},{48,32},{64,48},{80,64},{96,80},{112,96},{128,112},... | collective-permute-start | bytes 442376 | tf_op jit(solution)/shard_map/ppermute | solution.py:47
  297.3 11.8 %collective-permute-start.9 = (bf16[64,2304]{1,0:T(8,128)(2,1)S(1)}, bf16[64,2304]{1,0:T(8,128)(2,1)S(1)}, u32[]{:S(2)}, u32[]{:S(2)}) collective-permute-start(bf16[64,2304]{1,0:T(8,128)(2,1)S(1)} %pad_maximum_fusion.1), channel_id=1, source_target_pairs={{0,1},{1,0},{2,3},{3,2},{4,5},{5,4},{6,7},{7,6},{8,9},{9,8},{10,11... | collective-permute-start | bytes 884744 | tf_op jit(solution)/shard_map/ppermute | solution.py:41
  329.9 16.7 %all-to-all-start.17 = ((bf16[16,40,128]{2,1,0:T(8,128)(2,1)}), bf16[16,40,128]{2,1,0:T(8,128)(2,1)S(1)}, u32[]{:S(2)}, u32[]{:S(2)}) async-start(bf16[16,40,128]{2,1,0:T(8,128)(2,1)} %broadcast_in_dim.317), calls=%async_computation.17 | async-start | bytes 327680 | tf_op jit(solution)/shard_map/all_to_all | solution.py:22

commit v3 on v1

--- a/solution.py
+++ b/solution.py
@@ -231,6 +231,16 @@
         size = value.shape[axis] // 2
         return lax.dynamic_slice_in_dim(value, which * size, size, axis)
 
+    stacked, root_sent, map_mid, map_low, mass_cols = lax.optimization_barrier(
+        (
+            side_by_side(modes_root, modes_mid, modes_low),
+            factor_root[0],
+            map_mid,
+            map_low,
+            mass_cols,
+        )
+    )
+
     column = mass_cols - (owner - 1) * local_blocks
     place = column // local_blocks
     block = column % local_blocks
@@ -282,9 +292,16 @@
     def cut(flat, target, count):
         return [(target == i, flat[:, i * BLOCK : (i + 1) * BLOCK]) for i in range(count)]
 
-    stacked = side_by_side(modes_root, modes_mid, modes_low)
+    layer = lax.axis_index("z")
+    t_own = t_low - first_mid
     before, after = neighbours(stacked)
-    factors_root = (factor_root[0], swap(factor_root[0]))
+    root_received = swap(root_sent)
+    before, after, root_received, t_mid, t_low, t_own, column_after, layer = (
+        lax.optimization_barrier(
+            (before, after, root_received, t_mid, t_low, t_own, column_after, layer)
+        )
+    )
+    factors_root = (factor_root[0], root_received)
     window = jnp.concatenate([before, stacked, after], axis=1)
     z_part = mass_partial(window, column, mass_vals).astype(BF16)
 
@@ -299,11 +316,7 @@
         2, layers, modes // layers, w_root + w_own
     )
     z_part = jnp.transpose(z_part, (1, 0, 2, 3)).reshape(2 * layers, *z_part.shape[2:])
-    layer = lax.axis_index("z")
-    t_own = t_low - first_mid
-    z_part, t_mid, t_low, t_own, column_after, core, layer = lax.optimization_barrier(
-        (z_part, t_mid, t_low, t_own, column_after, core, layer)
-    )
+    z_part, core = lax.optimization_barrier((z_part, core))
     stacks, received = split_nodes(core, factor_low, factor_mid, update_low, update_mid)
     (z_mine,) = scatter_sum(z_part, FRONT)
     f_low, f_mid, u_low, u_mid = unpacked(stacks, received)
@@ -324,13 +337,14 @@
     acc_root = acc_root + placed(term, t_mid, b_root)
 
     half_modes = modes // 2
-    z_root, t_mid, core = lax.optimization_barrier((z[:, :mid_at], t_mid, core))
+    acc_root, t_mid, core = lax.optimization_barrier((acc_root, t_mid, core))
 
     def of_modes(value, which):
         return lax.dynamic_slice_in_dim(value, which * half_modes, half_modes, 0)
 
     acc_root = of_modes(acc_root, core) + swap(of_modes(acc_root, 1 - core))
-    right = (of_modes(z_root, core).astype(F32) - acc_root).astype(BF16)
+    z_root = lax.dynamic_slice(z, (core * half_modes, 0), (half_modes, mid_at))
+    right = (z_root.astype(F32) - acc_root).astype(BF16)
 
     def by_core(mine, other):
         return jnp.concatenate(

time: 345 us -> 346 us (level)
  blocking collectives: 239 us -> 250 us
  starting transfers between devices: 61.2 us -> 54.6 us
    all_to_all x17 -> x18, blocking collectives: 239 us -> 250 us  [exchange(): return lax.optimization_barrier((lax.all_to_all(pieces, axis, 0, 0), *held))]
    ppermute x2, waiting for transfers between devices: 6.25 us -> 1.62 us  [neighbours(): lax.ppermute(flat, 'subtree', [(i + 1, i) for i in range(count - 1)])]
    ppermute x5, starting transfers between devices: 40.6 us -> 36.7 us  [swap(): return lax.ppermute(value, 'core', [(0, 1), (1, 0)])]
    all_to_all x2 -> x1, starting transfers between devices: 10.5 us -> 7.08 us  [exchange(): return lax.optimization_barrier((lax.all_to_all(pieces, axis, 0, 0), *held))]
    all_to_all x2 -> x1, waiting for transfers between devices: 8.96 us -> 8.96 us  [exchange(): return lax.optimization_barrier((lax.all_to_all(pieces, axis, 0, 0), *held))]
  transfers between devices with their start and end apart: 11 -> 10, of which waited for: 7 -> 8; matrix products, arithmetic and copies ran while one was open for 1% -> 1% of each run, Pallas kernels for 0% -> 0%
where the time goes in v3:
time: 346 us; the launch traced here: 345 us
  blocking collectives  250 us (72%)
  starting transfers between devices  54.6 us (16%)
  waiting for transfers between devices  15.6 us (5%)
  Pallas kernels  6.51 us (2%)
  local copies, waits for them, and re-layouts  6.23 us (2%)
  matrix products  5.65 us (2%)
  other arithmetic  4.3 us (1%)
    all_to_all x18, blocking collectives, exchange(): return lax.optimization_barrier((lax.all_to_all(pieces, axis, 0, 0), *held))  250 us
    ppermute x5, starting transfers between devices, swap(): return lax.ppermute(value, 'core', [(0, 1), (1, 0)])  36.7 us
    all_to_all x1, waiting for transfers between devices, exchange(): return lax.optimization_barrier((lax.all_to_all(pieces, axis, 0, 0), *held))  8.96 us
    ppermute x2, starting transfers between devices, neighbours(): lax.ppermute(flat, 'subtree', [(i, i + 1) for i in range(count - 1)])  8.23 us
    all_to_all x1, starting transfers between devices, exchange(): return lax.optimization_barrier((lax.all_to_all(pieces, axis, 0, 0), *held))  7.08 us
  transfers between devices with their start and end apart: 10, of which 8 were waited for; matrix products, arithmetic and copies ran while one was open for 1% of the time, Pallas kernels for 0%

profile of v3, /device:TPU:1, one launch (start us, length us, event | category | flops | bytes accessed | tf_op | source)
XLA Modules:
  0.0 344.8 jit_solution(12700900965091232808)
XLA Ops:
  0.6 1.7 side_by_side.1
  2.3 8.7 %collective-permute-start.2 = (bf16[768,384]{1,0:T(8,128)(2,1)}, bf16[768,384]{1,0:T(8,128)(2,1)S(1)}, u32[]{:S(2)}, u32[]{:S(2)}) collective-permute-start(bf16[768,384]{1,0:T(8,128)(2,1)} %bitcast.179), channel_id=1, source_target_pairs={{0,1},{1,0},{2,3},{3,2},{4,5},{5,4},{6,7},{7,6},{8,9},{9,8},{10,11... | collective-permute-start | bytes 1769480 | tf_op jit(solution)/shard_map/ppermute | solution.py:41
  11.1 1.3 collective-permute-start.1
  12.4 4.0 %collective-permute-start = (bf16[64,1920]{1,0:T(8,128)(2,1)}, bf16[64,1920]{1,0:T(8,128)(2,1)S(1)}, u32[]{:S(2)}, u32[]{:S(2)}) collective-permute-start(bf16[64,1920]{1,0:T(8,128)(2,1)} %side_by_side.1), channel_id=1, source_target_pairs={{0,16},{16,32},{32,48},{48,64},{64,80},{80,96},{96,112},{112,128},... | collective-permute-start | bytes 737288 | tf_op jit(solution)/shard_map/ppermute | solution.py:46
  16.4 0.7 fusion.72
  17.1 1.2 constant_dynamic-slice_fusion.2
  19.0 0.7 broadcast_subtract_fusion
  19.7 1.0 collective-permute-done.1
  20.7 1.0 collective-permute-done
  21.7 1.1 copy_bitcast_fusion.1
  24.1 3.0 pack.1
  27.2 3.1 collective-permute-start.3
  30.2 17.2 %all_to_all.95 = bf16[16,8,1152]{2,1,0:T(8,128)(2,1)S(1)} all-to-all(bf16[16,8,1152]{2,1,0:T(8,128)(2,1)S(1)} %bitcast.187), channel_id=1, replica_groups=mesh['subtree'=32,'z'=8,'core'=2] {'z','core'}, dimensions={0} | all-to-all | bytes 589824 | tf_op jit(solution)/shard_map/all_to_all | solution.py:22
  47.5 11.1 %all_to_all.96 = bf16[8,8,1152]{2,1,0:T(8,128)(2,1)S(1)} all-to-all(bf16[8,8,1152]{2,1,0:T(8,128)(2,1)S(1)} %broadcast_in_dim.269), channel_id=1, replica_groups=mesh['subtree'=32,'z'=8,'core'=2] {'z'}, dimensions={0} | all-to-all | bytes 294912 | tf_op jit(solution)/shard_map/all_to_all | solution.py:22
  59.3 1.1 unpack.1
  60.3 1.7 fusion
  62.0 21.3 %all_to_all.97 = bf16[32,8,512]{2,1,0:T(8,128)(2,1)S(1)} all-to-all(bf16[32,8,512]{2,1,0:T(8,128)(2,1)S(1)} %bitcast.189), channel_id=1, replica_groups=mesh['subtree'=32,'z'=8,'core'=2] {'subtree'}, dimensions={0} | all-to-all | bytes 524288 | tf_op jit(solution)/shard_map/all_to_all | solution.py:22
  83.4 14.8 %all_to_all.98 = bf16[32,8,512]{2,1,0:T(8,128)(2,1)S(1)} all-to-all(bf16[32,8,512]{2,1,0:T(8,128)(2,1)S(1)} %broadcast_in_dim.270), channel_id=1, replica_groups=mesh['subtree'=32,'z'=8,'core'=2] {'subtree'}, dimensions={0} | all-to-all | bytes 524288 | tf_op jit(solution)/shard_map/all_to_all | solution.py:22
  98.6 12.3 %all_to_all.99 = bf16[8,2,64,128]{3,2,1,0:T(8,128)(2,1)S(1)} all-to-all(bf16[8,2,64,128]{3,2,1,0:T(8,128)(2,1)S(1)} %broadcast_in_dim.271), channel_id=1, replica_groups=mesh['subtree'=32,'z'=8,'core'=2] {'z'}, dimensions={0} | all-to-all | bytes 524288 | tf_op jit(solution)/shard_map/all_to_all | solution.py:22
  111.4 14.8 %all_to_all.100 = bf16[32,8,256]{2,1,0:T(8,128)(2,1)S(1)} all-to-all(bf16[32,8,256]{2,1,0:T(8,128)(2,1)S(1)} %bitcast.197), channel_id=1, replica_groups=mesh['subtree'=32,'z'=8,'core'=2] {'subtree'}, dimensions={0} | all-to-all | bytes 262144 | tf_op jit(solution)/shard_map/all_to_all | solution.py:22
  126.3 12.7 %all_to_all.101 = bf16[32,8,256]{2,1,0:T(8,128)(2,1)S(1)} all-to-all(bf16[32,8,256]{2,1,0:T(8,128)(2,1)S(1)} %broadcast_in_dim.278), channel_id=1, replica_groups=mesh['subtree'=32,'z'=8,'core'=2] {'subtree'}, dimensions={0} | all-to-all | bytes 262144 | tf_op jit(solution)/shard_map/all_to_all | solution.py:22
  139.2 10.4 %all_to_all.102 = bf16[8,1,64,128]{3,2,1,0:T(8,128)(2,1)S(1)} all-to-all(bf16[8,1,64,128]{3,2,1,0:T(8,128)(2,1)S(1)} %broadcast_in_dim.279), channel_id=1, replica_groups=mesh['subtree'=32,'z'=8,'core'=2] {'z'}, dimensions={0} | all-to-all | bytes 262144 | tf_op jit(solution)/shard_map/all_to_all | solution.py:22
  149.8 9.1 %collective-permute-start.4 = (f32[32,384]{1,0:T(8,128)S(1)}, f32[32,384]{1,0:T(8,128)S(1)}, u32[]{:S(2)}, u32[]{:S(2)}) collective-permute-start(f32[32,384]{1,0:T(8,128)S(1)} %constant_dynamic-slice_fusion), channel_id=1, source_target_pairs={{0,1},{1,0},{2,3},{3,2},{4,5},{5,4},{6,7},{7,6},{8,9},{9,8},{10,11... | collective-permute-start | bytes 147464 | tf_op jit(solution)/shard_map/ppermute | solution.py:41
  158.9 0.9 collective-permute-done.4
  160.4 12.4 %all_to_all.103 = bf16[32,8,256]{2,1,0:T(8,128)(2,1)S(1)} all-to-all(bf16[32,8,256]{2,1,0:T(8,128)(2,1)S(1)} %concatenate.64), channel_id=1, replica_groups=mesh['subtree'=32,'z'=8,'core'=2] {'subtree'}, dimensions={0} | all-to-all | bytes 262144 | tf_op jit(solution)/shard_map/all_to_all | solution.py:22
  172.9 13.3 %all_to_all.104 = bf16[32,8,256]{2,1,0:T(8,128)(2,1)S(1)} all-to-all(bf16[32,8,256]{2,1,0:T(8,128)(2,1)S(1)} %broadcast_in_dim.287), channel_id=1, replica_groups=mesh['subtree'=32,'z'=8,'core'=2] {'subtree'}, dimensions={0} | all-to-all | bytes 262144 | tf_op jit(solution)/shard_map/all_to_all | solution.py:22
  186.8 11.0 %all_to_all.105 = bf16[8,32,384]{2,1,0:T(8,128)(2,1)S(1)} all-to-all(bf16[8,32,384]{2,1,0:T(8,128)(2,1)S(1)} %broadcast_in_dim.288), channel_id=1, replica_groups=mesh['subtree'=32,'z'=8,'core'=2] {'z'}, dimensions={0} | all-to-all | bytes 393216 | tf_op jit(solution)/shard_map/all_to_all | solution.py:22
  197.8 5.8 %collective-permute-start.5 = (f32[32,384]{1,0:T(8,128)S(1)}, f32[32,384]{1,0:T(8,128)S(1)}, u32[]{:S(2)}, u32[]{:S(2)}) collective-permute-start(f32[32,384]{1,0:T(8,128)S(1)} %convert_reduce_fusion.3), channel_id=1, source_target_pairs={{0,1},{1,0},{2,3},{3,2},{4,5},{5,4},{6,7},{7,6},{8,9},{9,8},{10,11... | collective-permute-start | bytes 147464 | tf_op jit(solution)/shard_map/ppermute | solution.py:41
  203.6 0.8 collective-permute-done.5
  204.7 12.3 %all_to_all.106 = bf16[32,8,256]{2,1,0:T(8,128)(2,1)S(1)} all-to-all(bf16[32,8,256]{2,1,0:T(8,128)(2,1)S(1)} %bitcast.194), channel_id=1, replica_groups=mesh['subtree'=32,'z'=8,'core'=2] {'subtree'}, dimensions={0} | all-to-all | bytes 262144 | tf_op jit(solution)/shard_map/all_to_all | solution.py:22
  217.0 13.3 %all_to_all.107 = bf16[32,8,256]{2,1,0:T(8,128)(2,1)S(1)} all-to-all(bf16[32,8,256]{2,1,0:T(8,128)(2,1)S(1)} %broadcast_in_dim.296), channel_id=1, replica_groups=mesh['subtree'=32,'z'=8,'core'=2] {'subtree'}, dimensions={0} | all-to-all | bytes 262144 | tf_op jit(solution)/shard_map/all_to_all | solution.py:22
  230.6 11.8 %all_to_all.108 = bf16[8,64,256]{2,1,0:T(8,128)(2,1)S(1)} all-to-all(bf16[8,64,256]{2,1,0:T(8,128)(2,1)S(1)} %broadcast_in_dim.297), channel_id=1, replica_groups=mesh['subtree'=32,'z'=8,'core'=2] {'z'}, dimensions={0} | all-to-all | bytes 524288 | tf_op jit(solution)/shard_map/all_to_all | solution.py:22
  242.8 13.6 %all_to_all.109 = bf16[32,8,512]{2,1,0:T(8,128)(2,1)S(1)} all-to-all(bf16[32,8,512]{2,1,0:T(8,128)(2,1)S(1)} %bitcast.190), channel_id=1, replica_groups=mesh['subtree'=32,'z'=8,'core'=2] {'subtree'}, dimensions={0} | all-to-all | bytes 524288 | tf_op jit(solution)/shard_map/all_to_all | solution.py:22
  256.5 13.8 %all_to_all.110 = bf16[32,8,512]{2,1,0:T(8,128)(2,1)S(1)} all-to-all(bf16[32,8,512]{2,1,0:T(8,128)(2,1)S(1)} %broadcast_in_dim.309), channel_id=1, replica_groups=mesh['subtree'=32,'z'=8,'core'=2] {'subtree'}, dimensions={0} | all-to-all | bytes 524288 | tf_op jit(solution)/shard_map/all_to_all | solution.py:22
  270.6 14.7 %all_to_all.111 = bf16[8,64,512]{2,1,0:T(8,128)(2,1)S(1)} all-to-all(bf16[8,64,512]{2,1,0:T(8,128)(2,1)S(1)} %broadcast_in_dim.310), channel_id=1, replica_groups=mesh['subtree'=32,'z'=8,'core'=2] {'z'}, dimensions={0} | all-to-all | bytes 1048576 | tf_op jit(solution)/shard_map/all_to_all | solution.py:22
  285.4 1.3 collective-permute-start.7
  286.7 4.2 %collective-permute-start.6 = (bf16[64,1152]{1,0:T(8,128)(2,1)S(1)}, bf16[64,1152]{1,0:T(8,128)(2,1)S(1)}, u32[]{:S(2)}, u32[]{:S(2)}) collective-permute-start(bf16[64,1152]{1,0:T(8,128)(2,1)S(1)} %pad_maximum_fusion.2), channel_id=1, source_target_pairs={{0,16},{16,32},{32,48},{48,64},{64,80},{80,96},{96,112},{112,128},... | collective-permute-start | bytes 442376 | tf_op jit(solution)/shard_map/ppermute | solution.py:46
  291.1 0.7 collective-permute-done.7
  291.8 1.2 collective-permute-done.6
  293.0 10.0 %collective-permute-start.8 = (bf16[64,2304]{1,0:T(8,128)(2,1)S(1)}, bf16[64,2304]{1,0:T(8,128)(2,1)S(1)}, u32[]{:S(2)}, u32[]{:S(2)}) collective-permute-start(bf16[64,2304]{1,0:T(8,128)(2,1)S(1)} %pad_maximum_fusion.1), channel_id=1, source_target_pairs={{0,1},{1,0},{2,3},{3,2},{4,5},{5,4},{6,7},{7,6},{8,9},{9,8},{10,11... | collective-permute-start | bytes 884744 | tf_op jit(solution)/shard_map/ppermute | solution.py:41
  303.1 1.1 collective-permute-done.8
  306.0 18.9 %all_to_all.112 = bf16[32,40,128]{2,1,0:T(8,128)(2,1)S(1)} all-to-all(bf16[32,40,128]{2,1,0:T(8,128)(2,1)S(1)} %broadcast_in_dim.313), channel_id=1, replica_groups=mesh['subtree'=32,'z'=8,'core'=2] {'subtree'}, dimensions={0} | all-to-all | bytes 655360 | tf_op jit(solution)/shard_map/all_to_all | solution.py:22
  325.1 0.7 copy.55
  325.9 0.8 copy.56
  326.7 0.7 broadcast_in_dim.315
  327.3 7.1 %all-to-all-start.18 = ((bf16[16,40,128]{2,1,0:T(8,128)(2,1)}), bf16[16,40,128]{2,1,0:T(8,128)(2,1)S(1)}, u32[]{:S(2)}, u32[]{:S(2)}) async-start(bf16[16,40,128]{2,1,0:T(8,128)(2,1)} %broadcast_in_dim.315), calls=%async_computation.18 | async-start | bytes 327680 | tf_op jit(solution)/shard_map/all_to_all | solution.py:22
  335.1 9.0 %all-to-all-done.18.grams = bf16[16,40,128]{2,1,0:T(8,128)(2,1)S(1)} async-done(((bf16[16,40,128]{2,1,0:T(8,128)(2,1)}), bf16[16,40,128]{2,1,0:T(8,128)(2,1)S(1)}, u32[]{:S(2)}, u32[]{:S(2)}) %all-to-all-start.18) | async-done | bytes 163872 | tf_op jit(solution)/shard_map/all_to_all | solution.py:22
  344.0 0.7 unpaired.1
  (122 shorter events, 8.6 us)
Async XLA Ops:
  0.6 22.8 %copy-start = (bf16[15,1,128,128]{3,2,1,0:T(8,128)(2,1)S(1)}, bf16[15,1,128,128]{3,2,1,0:T(8,128)(2,1)}, u32[]{:S(2)}) copy-start(bf16[15,1,128,128]{3,2,1,0:T(8,128)(2,1)} %param.22) | copy-start | bytes 1474564
  2.3 19.4 %collective-permute-start.2 = (bf16[768,384]{1,0:T(8,128)(2,1)}, bf16[768,384]{1,0:T(8,128)(2,1)S(1)}, u32[]{:S(2)}, u32[]{:S(2)}) collective-permute-start(bf16[768,384]{1,0:T(8,128)(2,1)} %bitcast.179), channel_id=1, source_target_pairs={{0,1},{1,0},{2,3},{3,2},{4,5},{5,4},{6,7},{7,6},{8,9},{9,8},{10,11... | collective-permute-start | bytes 1769480 | tf_op jit(solution)/shard_map/ppermute | solution.py:41
  11.1 9.6 %collective-permute-start.1 = (bf16[64,1920]{1,0:T(8,128)(2,1)}, bf16[64,1920]{1,0:T(8,128)(2,1)S(1)}, u32[]{:S(2)}, u32[]{:S(2)}) collective-permute-start(bf16[64,1920]{1,0:T(8,128)(2,1)} %side_by_side.1), channel_id=1, source_target_pairs={{16,0},{32,16},{48,32},{64,48},{80,64},{96,80},{112,96},{128,112},... | collective-permute-start | bytes 737288 | tf_op jit(solution)/shard_map/ppermute | solution.py:47
  12.4 9.3 %collective-permute-start = (bf16[64,1920]{1,0:T(8,128)(2,1)}, bf16[64,1920]{1,0:T(8,128)(2,1)S(1)}, u32[]{:S(2)}, u32[]{:S(2)}) collective-permute-start(bf16[64,1920]{1,0:T(8,128)(2,1)} %side_by_side.1), channel_id=1, source_target_pairs={{0,16},{16,32},{32,48},{48,64},{64,80},{80,96},{96,112},{112,128},... | collective-permute-start | bytes 737288 | tf_op jit(solution)/shard_map/ppermute | solution.py:46
  27.2 32.1 %collective-permute-start.3 = (bf16[2304,256]{1,0:T(8,128)(2,1)}, bf16[2304,256]{1,0:T(8,128)(2,1)S(1)}, u32[]{:S(2)}, u32[]{:S(2)}) collective-permute-start(bf16[2304,256]{1,0:T(8,128)(2,1)} %get-tuple-element.95), channel_id=1, source_target_pairs={{0,1},{1,0},{2,3},{3,2},{4,5},{5,4},{6,7},{7,6},{8,9},{9,8},{10,11... | collective-permute-start | bytes 3538952 | tf_op jit(solution)/shard_map/ppermute | solution.py:41
  58.6 0.6 copy-start.6
  62.0 36.2 %copy-start.3 = (bf16[2,2,128,512]{3,2,1,0:T(8,128)(2,1)S(1)}, bf16[2,2,128,512]{3,2,1,0:T(8,128)(2,1)}, u32[]{:S(2)}) copy-start(bf16[2,2,128,512]{3,2,1,0:T(8,128)(2,1)} %get-tuple-element.107) | copy-start | bytes 1572868
  98.2 12.8 %copy-start.7 = (bf16[8,8,1152]{2,1,0:T(8,128)(2,1)S(1)}, bf16[8,8,1152]{2,1,0:T(8,128)(2,1)}, u32[]{:S(2)}) copy-start(bf16[8,8,1152]{2,1,0:T(8,128)(2,1)} %copy-done.6) | copy-start | bytes 442372
  98.2 12.9 %copy-start.2 = (bf16[2,1,512,256]{3,2,1,0:T(8,128)(2,1)S(1)}, bf16[2,1,512,256]{3,2,1,0:T(8,128)(2,1)}, u32[]{:S(2)}) copy-start(bf16[2,1,512,256]{3,2,1,0:T(8,128)(2,1)} %get-tuple-element.114) | copy-start | bytes 1572868
  110.9 28.1 %copy-start.4 = (bf16[2,1,128,512]{3,2,1,0:T(8,128)(2,1)S(1)}, bf16[2,1,128,512]{3,2,1,0:T(8,128)(2,1)}, u32[]{:S(2)}) copy-start(bf16[2,1,128,512]{3,2,1,0:T(8,128)(2,1)} %get-tuple-element.119) | copy-start | bytes 786436
  126.2 33.6 %copy-start.5 = (bf16[1,768,384]{2,1,0:T(8,128)(2,1)S(1)}, bf16[1,768,384]{2,1,0:T(8,128)(2,1)}, u32[]{:S(2)}) copy-start(bf16[1,768,384]{2,1,0:T(8,128)(2,1)} %param.15) | copy-start | bytes 1769476
  149.8 10.0 %collective-permute-start.4 = (f32[32,384]{1,0:T(8,128)S(1)}, f32[32,384]{1,0:T(8,128)S(1)}, u32[]{:S(2)}, u32[]{:S(2)}) collective-permute-start(f32[32,384]{1,0:T(8,128)S(1)} %constant_dynamic-slice_fusion), channel_id=1, source_target_pairs={{0,1},{1,0},{2,3},{3,2},{4,5},{5,4},{6,7},{7,6},{8,9},{9,8},{10,11... | collective-permute-start | bytes 147464 | tf_op jit(solution)/shard_map/ppermute | solution.py:41
  197.8 6.6 %collective-permute-start.5 = (f32[32,384]{1,0:T(8,128)S(1)}, f32[32,384]{1,0:T(8,128)S(1)}, u32[]{:S(2)}, u32[]{:S(2)}) collective-permute-start(f32[32,384]{1,0:T(8,128)S(1)} %convert_reduce_fusion.3), channel_id=1, source_target_pairs={{0,1},{1,0},{2,3},{3,2},{4,5},{5,4},{6,7},{7,6},{8,9},{9,8},{10,11... | collective-permute-start | bytes 147464 | tf_op jit(solution)/shard_map/ppermute | solution.py:41
  242.8 27.5 %copy-start.1 = (bf16[2,2,512,256]{3,2,1,0:T(8,128)(2,1)S(1)}, bf16[2,2,512,256]{3,2,1,0:T(8,128)(2,1)}, u32[]{:S(2)}) copy-start(bf16[2,2,512,256]{3,2,1,0:T(8,128)(2,1)} %get-tuple-element.100) | copy-start | bytes 3145732
  285.4 6.4 %collective-permute-start.7 = (bf16[64,1152]{1,0:T(8,128)(2,1)S(1)}, bf16[64,1152]{1,0:T(8,128)(2,1)S(1)}, u32[]{:S(2)}, u32[]{:S(2)}) collective-permute-start(bf16[64,1152]{1,0:T(8,128)(2,1)S(1)} %pad_maximum_fusion.2), channel_id=1, source_target_pairs={{16,0},{32,16},{48,32},{64,48},{80,64},{96,80},{112,96},{128,112},... | collective-permute-start | bytes 442376 | tf_op jit(solution)/shard_map/ppermute | solution.py:47
  286.7 6.3 %collective-permute-start.6 = (bf16[64,1152]{1,0:T(8,128)(2,1)S(1)}, bf16[64,1152]{1,0:T(8,128)(2,1)S(1)}, u32[]{:S(2)}, u32[]{:S(2)}) collective-permute-start(bf16[64,1152]{1,0:T(8,128)(2,1)S(1)} %pad_maximum_fusion.2), channel_id=1, source_target_pairs={{0,16},{16,32},{32,48},{48,64},{64,80},{80,96},{96,112},{112,128},... | collective-permute-start | bytes 442376 | tf_op jit(solution)/shard_map/ppermute | solution.py:46
  293.0 11.2 %collective-permute-start.8 = (bf16[64,2304]{1,0:T(8,128)(2,1)S(1)}, bf16[64,2304]{1,0:T(8,128)(2,1)S(1)}, u32[]{:S(2)}, u32[]{:S(2)}) collective-permute-start(bf16[64,2304]{1,0:T(8,128)(2,1)S(1)} %pad_maximum_fusion.1), channel_id=1, source_target_pairs={{0,1},{1,0},{2,3},{3,2},{4,5},{5,4},{6,7},{7,6},{8,9},{9,8},{10,11... | collective-permute-start | bytes 884744 | tf_op jit(solution)/shard_map/ppermute | solution.py:41
  327.3 16.7 %all-to-all-start.18 = ((bf16[16,40,128]{2,1,0:T(8,128)(2,1)}), bf16[16,40,128]{2,1,0:T(8,128)(2,1)S(1)}, u32[]{:S(2)}, u32[]{:S(2)}) async-start(bf16[16,40,128]{2,1,0:T(8,128)(2,1)} %broadcast_in_dim.315), calls=%async_computation.18 | async-start | bytes 327680 | tf_op jit(solution)/shard_map/all_to_all | solution.py:22

commit v4 on v3

--- a/solution.py
+++ b/solution.py
@@ -380,17 +380,19 @@
 
     y_own = jnp.concatenate([x_root, x_mid, x_low], axis=1)
     before, after = neighbours(y_own)
-    others = swap(jnp.concatenate([part[:, w_root:] for part in (before, y_own, after)], axis=1))
-    window = jnp.concatenate([before, y_own, after, others], axis=1)
-    my_part = mass_partial(window, column_after, mass_vals).astype(BF16)
-
-    other = others[:, w_own : 2 * w_own]
     own = y_own[:, w_root:]
+    other = swap(own)
     first = jnp.where(core == 0, own, other)
     second = jnp.where(core == 0, other, own)
     y_all = jnp.concatenate(
         [x_root, first[:, :w_mid], second[:, :w_mid], first[:, w_mid:], second[:, w_mid:]], axis=1
     )
+    before, after, other, y_all = lax.optimization_barrier((before, after, other, y_all))
+    others = swap(jnp.concatenate([before[:, w_root:], after[:, w_root:]], axis=1))
+    window = jnp.concatenate(
+        [before, y_own, after, others[:, :w_own], other, others[:, w_own:]], axis=1
+    )
+    my_part = mass_partial(window, column_after, mass_vals).astype(BF16)
 
     mass_part = jnp.einsum("jr,kr->jk", y_all, my_part, preferred_element_type=F32)
     size = modes // layers

time: 346 us -> 346 us (level)
    ppermute x5 -> x6, starting transfers between devices: 36.7 us -> 38.4 us  [swap(): return lax.ppermute(value, 'core', [(0, 1), (1, 0)])]
  transfers between devices with their start and end apart: 10 -> 11, of which waited for: 8 -> 7; matrix products, arithmetic and copies ran while one was open for 1% -> 1% of each run, Pallas kernels for 0% -> 0%
where the time goes in v4:
time: 346 us; the launch traced here: 345 us
  blocking collectives  249 us (72%)
  starting transfers between devices  56.3 us (16%)
  waiting for transfers between devices  14.4 us (4%)
  Pallas kernels  6.51 us (2%)
  local copies, waits for them, and re-layouts  6.24 us (2%)
  matrix products  5.66 us (2%)
  other arithmetic  4.3 us (1%)
    all_to_all x18, blocking collectives, exchange(): return lax.optimization_barrier((lax.all_to_all(pieces, axis, 0, 0), *held))  249 us
    ppermute x6, starting transfers between devices, swap(): return lax.ppermute(value, 'core', [(0, 1), (1, 0)])  38.4 us
    all_to_all x1, waiting for transfers between devices, exchange(): return lax.optimization_barrier((lax.all_to_all(pieces, axis, 0, 0), *held))  8.96 us
    ppermute x2, starting transfers between devices, neighbours(): lax.ppermute(flat, 'subtree', [(i, i + 1) for i in range(count - 1)])  8.23 us
    all_to_all x1, starting transfers between devices, exchange(): return lax.optimization_barrier((lax.all_to_all(pieces, axis, 0, 0), *held))  7.08 us
  transfers between devices with their start and end apart: 11, of which 7 were waited for; matrix products, arithmetic and copies ran while one was open for 1% of the time, Pallas kernels for 0%

profile of v4, /device:TPU:1, one launch (start us, length us, event | category | flops | bytes accessed | tf_op | source)
XLA Modules:
  0.0 344.6 jit_solution(448654635729064958)
XLA Ops:
  0.6 1.7 side_by_side.1
  2.3 8.7 %collective-permute-start.2 = (bf16[768,384]{1,0:T(8,128)(2,1)}, bf16[768,384]{1,0:T(8,128)(2,1)S(1)}, u32[]{:S(2)}, u32[]{:S(2)}) collective-permute-start(bf16[768,384]{1,0:T(8,128)(2,1)} %bitcast.179), channel_id=1, source_target_pairs={{0,1},{1,0},{2,3},{3,2},{4,5},{5,4},{6,7},{7,6},{8,9},{9,8},{10,11... | collective-permute-start | bytes 1769480 | tf_op jit(solution)/shard_map/ppermute | solution.py:41
  11.1 1.3 collective-permute-start.1
  12.4 4.0 %collective-permute-start = (bf16[64,1920]{1,0:T(8,128)(2,1)}, bf16[64,1920]{1,0:T(8,128)(2,1)S(1)}, u32[]{:S(2)}, u32[]{:S(2)}) collective-permute-start(bf16[64,1920]{1,0:T(8,128)(2,1)} %side_by_side.1), channel_id=1, source_target_pairs={{0,16},{16,32},{32,48},{48,64},{64,80},{80,96},{96,112},{112,128},... | collective-permute-start | bytes 737288 | tf_op jit(solution)/shard_map/ppermute | solution.py:46
  16.4 0.7 fusion.72
  17.1 1.2 constant_dynamic-slice_fusion.2
  19.0 0.7 broadcast_subtract_fusion
  19.7 1.0 collective-permute-done.1
  20.7 1.0 collective-permute-done
  21.7 1.1 copy_bitcast_fusion.1
  24.1 3.0 pack.1
  27.2 3.1 collective-permute-start.3
  30.2 17.2 %all_to_all.95 = bf16[16,8,1152]{2,1,0:T(8,128)(2,1)S(1)} all-to-all(bf16[16,8,1152]{2,1,0:T(8,128)(2,1)S(1)} %bitcast.187), channel_id=1, replica_groups=mesh['subtree'=32,'z'=8,'core'=2] {'z','core'}, dimensions={0} | all-to-all | bytes 589824 | tf_op jit(solution)/shard_map/all_to_all | solution.py:22
  47.5 11.1 %all_to_all.96 = bf16[8,8,1152]{2,1,0:T(8,128)(2,1)S(1)} all-to-all(bf16[8,8,1152]{2,1,0:T(8,128)(2,1)S(1)} %broadcast_in_dim.269), channel_id=1, replica_groups=mesh['subtree'=32,'z'=8,'core'=2] {'z'}, dimensions={0} | all-to-all | bytes 294912 | tf_op jit(solution)/shard_map/all_to_all | solution.py:22
  59.3 1.1 unpack.1
  60.3 1.7 fusion
  62.0 21.3 %all_to_all.97 = bf16[32,8,512]{2,1,0:T(8,128)(2,1)S(1)} all-to-all(bf16[32,8,512]{2,1,0:T(8,128)(2,1)S(1)} %bitcast.189), channel_id=1, replica_groups=mesh['subtree'=32,'z'=8,'core'=2] {'subtree'}, dimensions={0} | all-to-all | bytes 524288 | tf_op jit(solution)/shard_map/all_to_all | solution.py:22
  83.4 14.8 %all_to_all.98 = bf16[32,8,512]{2,1,0:T(8,128)(2,1)S(1)} all-to-all(bf16[32,8,512]{2,1,0:T(8,128)(2,1)S(1)} %broadcast_in_dim.270), channel_id=1, replica_groups=mesh['subtree'=32,'z'=8,'core'=2] {'subtree'}, dimensions={0} | all-to-all | bytes 524288 | tf_op jit(solution)/shard_map/all_to_all | solution.py:22
  98.6 12.3 %all_to_all.99 = bf16[8,2,64,128]{3,2,1,0:T(8,128)(2,1)S(1)} all-to-all(bf16[8,2,64,128]{3,2,1,0:T(8,128)(2,1)S(1)} %broadcast_in_dim.271), channel_id=1, replica_groups=mesh['subtree'=32,'z'=8,'core'=2] {'z'}, dimensions={0} | all-to-all | bytes 524288 | tf_op jit(solution)/shard_map/all_to_all | solution.py:22
  111.4 14.8 %all_to_all.100 = bf16[32,8,256]{2,1,0:T(8,128)(2,1)S(1)} all-to-all(bf16[32,8,256]{2,1,0:T(8,128)(2,1)S(1)} %bitcast.197), channel_id=1, replica_groups=mesh['subtree'=32,'z'=8,'core'=2] {'subtree'}, dimensions={0} | all-to-all | bytes 262144 | tf_op jit(solution)/shard_map/all_to_all | solution.py:22
  126.3 12.7 %all_to_all.101 = bf16[32,8,256]{2,1,0:T(8,128)(2,1)S(1)} all-to-all(bf16[32,8,256]{2,1,0:T(8,128)(2,1)S(1)} %broadcast_in_dim.278), channel_id=1, replica_groups=mesh['subtree'=32,'z'=8,'core'=2] {'subtree'}, dimensions={0} | all-to-all | bytes 262144 | tf_op jit(solution)/shard_map/all_to_all | solution.py:22
  139.2 10.4 %all_to_all.102 = bf16[8,1,64,128]{3,2,1,0:T(8,128)(2,1)S(1)} all-to-all(bf16[8,1,64,128]{3,2,1,0:T(8,128)(2,1)S(1)} %broadcast_in_dim.279), channel_id=1, replica_groups=mesh['subtree'=32,'z'=8,'core'=2] {'z'}, dimensions={0} | all-to-all | bytes 262144 | tf_op jit(solution)/shard_map/all_to_all | solution.py:22
  149.8 9.1 %collective-permute-start.4 = (f32[32,384]{1,0:T(8,128)S(1)}, f32[32,384]{1,0:T(8,128)S(1)}, u32[]{:S(2)}, u32[]{:S(2)}) collective-permute-start(f32[32,384]{1,0:T(8,128)S(1)} %constant_dynamic-slice_fusion), channel_id=1, source_target_pairs={{0,1},{1,0},{2,3},{3,2},{4,5},{5,4},{6,7},{7,6},{8,9},{9,8},{10,11... | collective-permute-start | bytes 147464 | tf_op jit(solution)/shard_map/ppermute | solution.py:41
  158.9 0.9 collective-permute-done.4
  160.4 12.4 %all_to_all.103 = bf16[32,8,256]{2,1,0:T(8,128)(2,1)S(1)} all-to-all(bf16[32,8,256]{2,1,0:T(8,128)(2,1)S(1)} %concatenate.63), channel_id=1, replica_groups=mesh['subtree'=32,'z'=8,'core'=2] {'subtree'}, dimensions={0} | all-to-all | bytes 262144 | tf_op jit(solution)/shard_map/all_to_all | solution.py:22
  172.9 13.3 %all_to_all.104 = bf16[32,8,256]{2,1,0:T(8,128)(2,1)S(1)} all-to-all(bf16[32,8,256]{2,1,0:T(8,128)(2,1)S(1)} %broadcast_in_dim.287), channel_id=1, replica_groups=mesh['subtree'=32,'z'=8,'core'=2] {'subtree'}, dimensions={0} | all-to-all | bytes 262144 | tf_op jit(solution)/shard_map/all_to_all | solution.py:22
  186.8 11.0 %all_to_all.105 = bf16[8,32,384]{2,1,0:T(8,128)(2,1)S(1)} all-to-all(bf16[8,32,384]{2,1,0:T(8,128)(2,1)S(1)} %broadcast_in_dim.288), channel_id=1, replica_groups=mesh['subtree'=32,'z'=8,'core'=2] {'z'}, dimensions={0} | all-to-all | bytes 393216 | tf_op jit(solution)/shard_map/all_to_all | solution.py:22
  197.8 5.8 %collective-permute-start.5 = (f32[32,384]{1,0:T(8,128)S(1)}, f32[32,384]{1,0:T(8,128)S(1)}, u32[]{:S(2)}, u32[]{:S(2)}) collective-permute-start(f32[32,384]{1,0:T(8,128)S(1)} %convert_reduce_fusion.3), channel_id=1, source_target_pairs={{0,1},{1,0},{2,3},{3,2},{4,5},{5,4},{6,7},{7,6},{8,9},{9,8},{10,11... | collective-permute-start | bytes 147464 | tf_op jit(solution)/shard_map/ppermute | solution.py:41
  203.6 0.8 collective-permute-done.5
  204.7 12.3 %all_to_all.106 = bf16[32,8,256]{2,1,0:T(8,128)(2,1)S(1)} all-to-all(bf16[32,8,256]{2,1,0:T(8,128)(2,1)S(1)} %bitcast.194), channel_id=1, replica_groups=mesh['subtree'=32,'z'=8,'core'=2] {'subtree'}, dimensions={0} | all-to-all | bytes 262144 | tf_op jit(solution)/shard_map/all_to_all | solution.py:22
  217.0 13.3 %all_to_all.107 = bf16[32,8,256]{2,1,0:T(8,128)(2,1)S(1)} all-to-all(bf16[32,8,256]{2,1,0:T(8,128)(2,1)S(1)} %broadcast_in_dim.296), channel_id=1, replica_groups=mesh['subtree'=32,'z'=8,'core'=2] {'subtree'}, dimensions={0} | all-to-all | bytes 262144 | tf_op jit(solution)/shard_map/all_to_all | solution.py:22
  230.6 11.8 %all_to_all.108 = bf16[8,64,256]{2,1,0:T(8,128)(2,1)S(1)} all-to-all(bf16[8,64,256]{2,1,0:T(8,128)(2,1)S(1)} %broadcast_in_dim.297), channel_id=1, replica_groups=mesh['subtree'=32,'z'=8,'core'=2] {'z'}, dimensions={0} | all-to-all | bytes 524288 | tf_op jit(solution)/shard_map/all_to_all | solution.py:22
  242.8 13.6 %all_to_all.109 = bf16[32,8,512]{2,1,0:T(8,128)(2,1)S(1)} all-to-all(bf16[32,8,512]{2,1,0:T(8,128)(2,1)S(1)} %bitcast.190), channel_id=1, replica_groups=mesh['subtree'=32,'z'=8,'core'=2] {'subtree'}, dimensions={0} | all-to-all | bytes 524288 | tf_op jit(solution)/shard_map/all_to_all | solution.py:22
  256.5 13.8 %all_to_all.110 = bf16[32,8,512]{2,1,0:T(8,128)(2,1)S(1)} all-to-all(bf16[32,8,512]{2,1,0:T(8,128)(2,1)S(1)} %broadcast_in_dim.309), channel_id=1, replica_groups=mesh['subtree'=32,'z'=8,'core'=2] {'subtree'}, dimensions={0} | all-to-all | bytes 524288 | tf_op jit(solution)/shard_map/all_to_all | solution.py:22
  270.6 14.7 %all_to_all.111 = bf16[8,64,512]{2,1,0:T(8,128)(2,1)S(1)} all-to-all(bf16[8,64,512]{2,1,0:T(8,128)(2,1)S(1)} %broadcast_in_dim.310), channel_id=1, replica_groups=mesh['subtree'=32,'z'=8,'core'=2] {'z'}, dimensions={0} | all-to-all | bytes 1048576 | tf_op jit(solution)/shard_map/all_to_all | solution.py:22
  285.4 1.3 collective-permute-start.7
  286.7 4.2 %collective-permute-start.6 = (bf16[64,1152]{1,0:T(8,128)(2,1)S(1)}, bf16[64,1152]{1,0:T(8,128)(2,1)S(1)}, u32[]{:S(2)}, u32[]{:S(2)}) collective-permute-start(bf16[64,1152]{1,0:T(8,128)(2,1)S(1)} %pad_maximum_fusion.2), channel_id=1, source_target_pairs={{0,16},{16,32},{32,48},{48,64},{64,80},{80,96},{96,112},{112,128},... | collective-permute-start | bytes 442376 | tf_op jit(solution)/shard_map/ppermute | solution.py:46
  291.0 9.4 %collective-permute-start.8 = (bf16[64,768]{1,0:T(8,128)(2,1)S(1)}, bf16[64,768]{1,0:T(8,128)(2,1)S(1)}, u32[]{:S(2)}, u32[]{:S(2)}) collective-permute-start(bf16[64,768]{1,0:T(8,128)(2,1)S(1)} %pad_maximum_fusion.5), channel_id=1, source_target_pairs={{0,1},{1,0},{2,3},{3,2},{4,5},{5,4},{6,7},{7,6},{8,9},{9,8},{10,11... | collective-permute-start | bytes 294920 | tf_op jit(solution)/shard_map/ppermute | solution.py:41
  300.6 0.7 collective-permute-done.8
  301.5 2.3 collective-permute-start.9
  303.9 1.0 collective-permute-done.9
  306.6 18.2 %all_to_all.112 = bf16[32,40,128]{2,1,0:T(8,128)(2,1)S(1)} all-to-all(bf16[32,40,128]{2,1,0:T(8,128)(2,1)S(1)} %broadcast_in_dim.313), channel_id=1, replica_groups=mesh['subtree'=32,'z'=8,'core'=2] {'subtree'}, dimensions={0} | all-to-all | bytes 655360 | tf_op jit(solution)/shard_map/all_to_all | solution.py:22
  325.0 0.7 copy.55
  325.7 0.8 copy.56
  326.5 0.7 broadcast_in_dim.315
  327.2 7.1 %all-to-all-start.18 = ((bf16[16,40,128]{2,1,0:T(8,128)(2,1)}), bf16[16,40,128]{2,1,0:T(8,128)(2,1)S(1)}, u32[]{:S(2)}, u32[]{:S(2)}) async-start(bf16[16,40,128]{2,1,0:T(8,128)(2,1)} %broadcast_in_dim.315), calls=%async_computation.18 | async-start | bytes 327680 | tf_op jit(solution)/shard_map/all_to_all | solution.py:22
  334.9 9.0 %all-to-all-done.18.grams = bf16[16,40,128]{2,1,0:T(8,128)(2,1)S(1)} async-done(((bf16[16,40,128]{2,1,0:T(8,128)(2,1)}), bf16[16,40,128]{2,1,0:T(8,128)(2,1)S(1)}, u32[]{:S(2)}, u32[]{:S(2)}) %all-to-all-start.18) | async-done | bytes 163872 | tf_op jit(solution)/shard_map/all_to_all | solution.py:22
  343.9 0.7 unpaired.1
  (128 shorter events, 8.7 us)
Async XLA Ops:
  0.6 22.8 %copy-start = (bf16[15,1,128,128]{3,2,1,0:T(8,128)(2,1)S(1)}, bf16[15,1,128,128]{3,2,1,0:T(8,128)(2,1)}, u32[]{:S(2)}) copy-start(bf16[15,1,128,128]{3,2,1,0:T(8,128)(2,1)} %param.22) | copy-start | bytes 1474564
  2.3 19.4 %collective-permute-start.2 = (bf16[768,384]{1,0:T(8,128)(2,1)}, bf16[768,384]{1,0:T(8,128)(2,1)S(1)}, u32[]{:S(2)}, u32[]{:S(2)}) collective-permute-start(bf16[768,384]{1,0:T(8,128)(2,1)} %bitcast.179), channel_id=1, source_target_pairs={{0,1},{1,0},{2,3},{3,2},{4,5},{5,4},{6,7},{7,6},{8,9},{9,8},{10,11... | collective-permute-start | bytes 1769480 | tf_op jit(solution)/shard_map/ppermute | solution.py:41
  11.1 9.6 %collective-permute-start.1 = (bf16[64,1920]{1,0:T(8,128)(2,1)}, bf16[64,1920]{1,0:T(8,128)(2,1)S(1)}, u32[]{:S(2)}, u32[]{:S(2)}) collective-permute-start(bf16[64,1920]{1,0:T(8,128)(2,1)} %side_by_side.1), channel_id=1, source_target_pairs={{16,0},{32,16},{48,32},{64,48},{80,64},{96,80},{112,96},{128,112},... | collective-permute-start | bytes 737288 | tf_op jit(solution)/shard_map/ppermute | solution.py:47
  12.4 9.3 %collective-permute-start = (bf16[64,1920]{1,0:T(8,128)(2,1)}, bf16[64,1920]{1,0:T(8,128)(2,1)S(1)}, u32[]{:S(2)}, u32[]{:S(2)}) collective-permute-start(bf16[64,1920]{1,0:T(8,128)(2,1)} %side_by_side.1), channel_id=1, source_target_pairs={{0,16},{16,32},{32,48},{48,64},{64,80},{80,96},{96,112},{112,128},... | collective-permute-start | bytes 737288 | tf_op jit(solution)/shard_map/ppermute | solution.py:46
  27.2 32.1 %collective-permute-start.3 = (bf16[2304,256]{1,0:T(8,128)(2,1)}, bf16[2304,256]{1,0:T(8,128)(2,1)S(1)}, u32[]{:S(2)}, u32[]{:S(2)}) collective-permute-start(bf16[2304,256]{1,0:T(8,128)(2,1)} %get-tuple-element.99), channel_id=1, source_target_pairs={{0,1},{1,0},{2,3},{3,2},{4,5},{5,4},{6,7},{7,6},{8,9},{9,8},{10,11... | collective-permute-start | bytes 3538952 | tf_op jit(solution)/shard_map/ppermute | solution.py:41
  58.6 0.6 copy-start.6
  62.0 36.2 %copy-start.3 = (bf16[2,2,128,512]{3,2,1,0:T(8,128)(2,1)S(1)}, bf16[2,2,128,512]{3,2,1,0:T(8,128)(2,1)}, u32[]{:S(2)}) copy-start(bf16[2,2,128,512]{3,2,1,0:T(8,128)(2,1)} %get-tuple-element.111) | copy-start | bytes 1572868
  98.2 12.8 %copy-start.7 = (bf16[8,8,1152]{2,1,0:T(8,128)(2,1)S(1)}, bf16[8,8,1152]{2,1,0:T(8,128)(2,1)}, u32[]{:S(2)}) copy-start(bf16[8,8,1152]{2,1,0:T(8,128)(2,1)} %copy-done.6) | copy-start | bytes 442372
  98.2 12.9 %copy-start.2 = (bf16[2,1,512,256]{3,2,1,0:T(8,128)(2,1)S(1)}, bf16[2,1,512,256]{3,2,1,0:T(8,128)(2,1)}, u32[]{:S(2)}) copy-start(bf16[2,1,512,256]{3,2,1,0:T(8,128)(2,1)} %get-tuple-element.118) | copy-start | bytes 1572868
  110.9 28.1 %copy-start.4 = (bf16[2,1,128,512]{3,2,1,0:T(8,128)(2,1)S(1)}, bf16[2,1,128,512]{3,2,1,0:T(8,128)(2,1)}, u32[]{:S(2)}) copy-start(bf16[2,1,128,512]{3,2,1,0:T(8,128)(2,1)} %get-tuple-element.123) | copy-start | bytes 786436
  126.2 33.6 %copy-start.5 = (bf16[1,768,384]{2,1,0:T(8,128)(2,1)S(1)}, bf16[1,768,384]{2,1,0:T(8,128)(2,1)}, u32[]{:S(2)}) copy-start(bf16[1,768,384]{2,1,0:T(8,128)(2,1)} %param.15) | copy-start | bytes 1769476
  149.8 10.0 %collective-permute-start.4 = (f32[32,384]{1,0:T(8,128)S(1)}, f32[32,384]{1,0:T(8,128)S(1)}, u32[]{:S(2)}, u32[]{:S(2)}) collective-permute-start(f32[32,384]{1,0:T(8,128)S(1)} %constant_dynamic-slice_fusion), channel_id=1, source_target_pairs={{0,1},{1,0},{2,3},{3,2},{4,5},{5,4},{6,7},{7,6},{8,9},{9,8},{10,11... | collective-permute-start | bytes 147464 | tf_op jit(solution)/shard_map/ppermute | solution.py:41
  197.8 6.6 %collective-permute-start.5 = (f32[32,384]{1,0:T(8,128)S(1)}, f32[32,384]{1,0:T(8,128)S(1)}, u32[]{:S(2)}, u32[]{:S(2)}) collective-permute-start(f32[32,384]{1,0:T(8,128)S(1)} %convert_reduce_fusion.3), channel_id=1, source_target_pairs={{0,1},{1,0},{2,3},{3,2},{4,5},{5,4},{6,7},{7,6},{8,9},{9,8},{10,11... | collective-permute-start | bytes 147464 | tf_op jit(solution)/shard_map/ppermute | solution.py:41
  242.8 27.5 %copy-start.1 = (bf16[2,2,512,256]{3,2,1,0:T(8,128)(2,1)S(1)}, bf16[2,2,512,256]{3,2,1,0:T(8,128)(2,1)}, u32[]{:S(2)}) copy-start(bf16[2,2,512,256]{3,2,1,0:T(8,128)(2,1)} %get-tuple-element.104) | copy-start | bytes 3145732
  285.4 16.0 %collective-permute-start.7 = (bf16[64,1152]{1,0:T(8,128)(2,1)S(1)}, bf16[64,1152]{1,0:T(8,128)(2,1)S(1)}, u32[]{:S(2)}, u32[]{:S(2)}) collective-permute-start(bf16[64,1152]{1,0:T(8,128)(2,1)S(1)} %pad_maximum_fusion.2), channel_id=1, source_target_pairs={{16,0},{32,16},{48,32},{64,48},{80,64},{96,80},{112,96},{128,112},... | collective-permute-start | bytes 442376 | tf_op jit(solution)/shard_map/ppermute | solution.py:47
  286.7 14.7 %collective-permute-start.6 = (bf16[64,1152]{1,0:T(8,128)(2,1)S(1)}, bf16[64,1152]{1,0:T(8,128)(2,1)S(1)}, u32[]{:S(2)}, u32[]{:S(2)}) collective-permute-start(bf16[64,1152]{1,0:T(8,128)(2,1)S(1)} %pad_maximum_fusion.2), channel_id=1, source_target_pairs={{0,16},{16,32},{32,48},{48,64},{64,80},{80,96},{96,112},{112,128},... | collective-permute-start | bytes 442376 | tf_op jit(solution)/shard_map/ppermute | solution.py:46
  291.0 10.4 %collective-permute-start.8 = (bf16[64,768]{1,0:T(8,128)(2,1)S(1)}, bf16[64,768]{1,0:T(8,128)(2,1)S(1)}, u32[]{:S(2)}, u32[]{:S(2)}) collective-permute-start(bf16[64,768]{1,0:T(8,128)(2,1)S(1)} %pad_maximum_fusion.5), channel_id=1, source_target_pairs={{0,1},{1,0},{2,3},{3,2},{4,5},{5,4},{6,7},{7,6},{8,9},{9,8},{10,11... | collective-permute-start | bytes 294920 | tf_op jit(solution)/shard_map/ppermute | solution.py:41
  301.5 3.3 collective-permute-start.9
  327.2 16.7 %all-to-all-start.18 = ((bf16[16,40,128]{2,1,0:T(8,128)(2,1)}), bf16[16,40,128]{2,1,0:T(8,128)(2,1)S(1)}, u32[]{:S(2)}, u32[]{:S(2)}) async-start(bf16[16,40,128]{2,1,0:T(8,128)(2,1)} %broadcast_in_dim.315), calls=%async_computation.18 | async-start | bytes 327680 | tf_op jit(solution)/shard_map/all_to_all | solution.py:22
